TPU v7x, 512 devices: a whole 4x8x8 slice. The times are simulated.
512 devices in a mesh: gx: 4 (over x), gy: 4 (over y_lo, core), gz: 32 (over y_hi, z).
Axes of the slice: x: 4, y: 8 (y_hi: 4, y_lo: 2; y = y_hi * 2 + y_lo), z: 8, core: 2. Of those that a mesh axis runs over, the one named last changes fastest.
Arguments:
- field_h: float32 [10, 128, 32, 512], P(None, 'gz', 'gy', 'gx'), may hold values from -6 to 6
- field_p: float32 [10, 128, 32, 512], P(None, 'gz', 'gy', 'gx'), may hold values from -6 to 6
- potential: float32 [128, 32, 512], P('gz', 'gy', 'gx'), may hold values from 0.25 to 2.5
- coupling: float32 [10, 10], replicated, may hold values from -2 to 2
- wt_cells: int32 [32, 4, 4, 8, 128], P('gz', 'gy', 'gx'), may hold values from 0 to 4095
- wt_coords: float32 [32, 4, 4, 8, 3, 128], P('gz', 'gy', 'gx'), may hold values from -1 to 1
- wt_patch: int32 [32, 4, 4, 8, 1], P('gz', 'gy', 'gx'), may hold values from 0 to 31; in each aligned block of 8 rows (0 to 7, 8 to 15, ..., all dimensions but the last counted through in order) at most 2 rows name the same one
- patch_coef: float32 [32, 10, 8, 64], P('gz'), may hold values from -0.75 to 0.75
- sph_points: int32 [65536], P(('gx', 'gy', 'gz')), may hold values from 0 to 65535, each once
- sph_cells: int32 [3, 65536], P(None, ('gx', 'gy', 'gz')), may hold values from 1 to 130, as said below
- sph_frac: float32 [3, 65536], P(None, ('gx', 'gy', 'gz')), may hold values from 0 to 1
Outputs:
- section_h: float32 [10, 128, 32, 512], P(None, 'gz', 'gy', 'gx')
- section_p: float32 [10, 128, 32, 512], P(None, 'gz', 'gy', 'gx')
- modes: float32 [32, 10, 961], P('gz')
Inputs may be any that keep to these rules, and one draw needn't show every extreme that they name: `wt_patch`: among the blocks of one device at most 2 name the same patch, and in some device exactly 2 do. `wt_cells`: cells are numbered (z * 8 + y) * 128 + x within the device's own block. `sph_points`: every sphere point s * 2048 + r appears exactly once. `sph_cells`: rows are z, y, x indices into the device's block extended by two cells on each side, counted from the outer edge of the extension; row z lies in 1 to 6, row y in 1 to 10, row x in 1 to 130.
All inputs are finite; a program needn't handle non-finite values.
Results may differ from a plain program's by a relative error of at most 0.0041.
Values may be sent and summed in bfloat16 or wider, within the bound.
No kernel may reach another device: no remote copies, remote signals or barrier semaphores. Data moves between devices by JAX's collectives and lax.ppermute only.
A program may use at most 64 MiB of HBM per device.

v0:
```python
import jax
import jax.numpy as jnp
import numpy as np
from jax import lax
from jax.sharding import PartitionSpec as P

NSPH = 32
LMAX = 30
NTHETA = 32
NPHI = 64
NANG = 2048


HALF_STEP = 0.125


def with_halo(block, sides, width):
    for axis, dim in sides:
        count = lax.axis_size(axis)
        forward = [(i, i + 1) for i in range(count - 1)]
        backward = [(target, source) for source, target in forward]
        low = lax.ppermute(
            lax.slice_in_dim(block, block.shape[dim] - width, None, axis=dim), axis, forward
        )
        high = lax.ppermute(lax.slice_in_dim(block, 0, width, axis=dim), axis, backward)
        block = jnp.concatenate([low, block, high], axis=dim)
    return block


def as_sent(value):
    return jax.tree.map(lambda a: a.astype(jnp.bfloat16) if a.dtype == jnp.float32 else a, value)


def cut_along(value, dim, size):
    dims = value.shape
    tiles = value.reshape(*dims[:dim], size, dims[dim] // size, *dims[dim + 1 :])
    return jnp.moveaxis(tiles, dim, 0)


def sum_at_owner(value, axis, dim):
    tiles = cut_along(value, dim, lax.axis_size(axis))
    arrived = lax.all_to_all(tiles, axis, split_axis=0, concat_axis=0, tiled=True)
    return arrived.sum(axis=0)


def sent_to_all(value, axis):
    size = lax.axis_size(axis)
    return lax.all_to_all(
        jnp.broadcast_to(value[None], (size, *value.shape)), axis, 0, 0, tiled=True
    )


def taken_together(value, axis):
    everything = sent_to_all(value, axis)
    return jnp.sum(everything, axis=0)


def harmonic_table(degree_max, polar_count, azimuth_count):
    polar_angle = np.pi * (np.arange(polar_count) + 0.5) / polar_count
    azimuth = 2.0 * np.pi * np.arange(azimuth_count) / azimuth_count
    cosine = np.cos(polar_angle)
    sine_polar = np.sin(polar_angle)
    legendre = np.zeros((degree_max + 1, degree_max + 1, polar_count))
    diagonal_term = np.full(polar_count, np.sqrt(0.25 / np.pi))
    for order_m in range(degree_max + 1):
        if order_m > 0:
            diagonal_term = (
                diagonal_term * sine_polar * np.sqrt((2.0 * order_m + 1.0) / (2.0 * order_m))
            )
        legendre[order_m, order_m] = diagonal_term
        if order_m < degree_max:
            legendre[order_m + 1, order_m] = cosine * np.sqrt(2.0 * order_m + 3.0) * diagonal_term
        for degree_l in range(order_m + 2, degree_max + 1):
            factor_a = np.sqrt(
                (4.0 * degree_l * degree_l - 1.0) / (degree_l * degree_l - order_m * order_m)
            )
            factor_b = np.sqrt(
                ((degree_l - 1.0) ** 2 - order_m * order_m) / (4.0 * (degree_l - 1.0) ** 2 - 1.0)
            )
            legendre[degree_l, order_m] = factor_a * (
                cosine * legendre[degree_l - 1, order_m]
                - factor_b * legendre[degree_l - 2, order_m]
            )
    columns = np.zeros((polar_count, azimuth_count, (degree_max + 1) ** 2))
    weight = sine_polar * np.pi / polar_count
    for degree_l in range(degree_max + 1):
        for order_m in range(-degree_l, degree_l + 1):
            radial = legendre[degree_l, abs(order_m)] * weight
            if order_m == 0:
                angular = np.ones(azimuth_count)
            elif order_m > 0:
                angular = np.sqrt(2.0) * np.cos(order_m * azimuth)
            else:
                angular = np.sqrt(2.0) * np.sin(-order_m * azimuth)
            columns[:, :, degree_l * degree_l + degree_l + order_m] = (
                radial[:, None] * angular[None, :]
            )
    flat_table = columns.reshape(polar_count * azimuth_count, -1).astype(np.float32)
    return jnp.asarray(flat_table).astype(jnp.bfloat16)


def chebyshev(values, terms):
    series = [jnp.ones_like(values), values]
    for index_k in range(2, terms):
        series.append(2.0 * values * series[-1] - series[-2])
    return jnp.stack(series[:terms])


def evaluate(coefficients, positions):
    terms = coefficients.shape[1]
    first = chebyshev(positions[0], terms)
    second = chebyshev(positions[1], terms)
    third = chebyshev(positions[2], terms)
    product = (second[:, None, :] * third[None, :, :]).reshape(terms * terms, -1)
    partial_sum = jnp.dot(
        coefficients.reshape(-1, terms * terms),
        product,
        precision=lax.Precision.HIGHEST,
        preferred_element_type=jnp.float32,
    )
    partial_sum = partial_sum.reshape(coefficients.shape[0], terms, -1)
    return jnp.einsum("aip,ip->ap", partial_sum, first, precision=lax.Precision.HIGHEST)


def laplace(padded):
    centre = padded[..., 2:-2, 2:-2, 2:-2]
    along_z = (
        -padded[..., 4:, 2:-2, 2:-2]
        + 16.0 * padded[..., 3:-1, 2:-2, 2:-2]
        + 16.0 * padded[..., 1:-3, 2:-2, 2:-2]
        - padded[..., :-4, 2:-2, 2:-2]
    )
    along_y = (
        -padded[..., 2:-2, 4:, 2:-2]
        + 16.0 * padded[..., 2:-2, 3:-1, 2:-2]
        + 16.0 * padded[..., 2:-2, 1:-3, 2:-2]
        - padded[..., 2:-2, :-4, 2:-2]
    )
    along_x = (
        -padded[..., 2:-2, 2:-2, 4:]
        + 16.0 * padded[..., 2:-2, 2:-2, 3:-1]
        + 16.0 * padded[..., 2:-2, 2:-2, 1:-3]
        - padded[..., 2:-2, 2:-2, :-4]
    )
    return (along_z + along_y + along_x - 90.0 * centre) / 12.0


def trilinear(flat_field, span_y, span_x, corner, fraction):
    summed = jnp.zeros((flat_field.shape[0], corner.shape[1]), jnp.float32)
    for step_z in (0, 1):
        weight_z = fraction[0] if step_z else 1.0 - fraction[0]
        for step_y in (0, 1):
            weight_y = fraction[1] if step_y else 1.0 - fraction[1]
            for step_x in (0, 1):
                weight_x = fraction[2] if step_x else 1.0 - fraction[2]
                position = (
                    ((corner[0] + step_z) * span_y + corner[1] + step_y) * span_x
                    + corner[2]
                    + step_x
                )
                summed = summed + (weight_z * weight_y * weight_x)[None, :] * jnp.take(
                    flat_field, position, axis=1
                )
    return summed


def shards(
    field_h,
    field_p,
    potential,
    coupling,
    wt_cells,
    wt_coords,
    wt_patch,
    patch_coef,
    sph_points,
    sph_cells,
    sph_frac,
):
    components, depth_cells, height_cells, width_cells = field_h.shape
    padded = with_halo(field_h, (("gx", 3), ("gy", 2), ("gz", 1)), 2)
    laplacian = laplace(padded)
    coupled = jnp.einsum("ab,bzyx->azyx", coupling, field_h, precision=lax.Precision.HIGHEST)
    right_side = laplacian - potential[None] * coupled
    positions = wt_coords[0, 0, 0]
    patch_ids = wt_patch[0, 0, 0, :, 0]
    cell_ids = wt_cells[0, 0, 0]
    slot_count = positions.shape[0]
    block_points = positions.shape[2]
    gz_count = lax.axis_size("gz")
    capacity = max(2, 2 * slot_count // gz_count)
    slot_order = jnp.arange(slot_count, dtype=jnp.int32)
    earlier = (patch_ids[:, None] == patch_ids[None, :]) & (
        slot_order[None, :] < slot_order[:, None]
    )
    slot_rank = jnp.sum(earlier.astype(jnp.int32), axis=1)
    outbox = (
        jnp.zeros((gz_count, capacity, 3, block_points), jnp.float32)
        .at[patch_ids, slot_rank]
        .set(positions)
    )
    coef_table = patch_coef[0]
    arrived = lax.all_to_all(
        outbox.astype(jnp.bfloat16), "gz", split_axis=0, concat_axis=0, tiled=True
    ).astype(outbox.dtype)
    items = arrived.shape[1]
    points = jnp.moveaxis(arrived, 2, 0).reshape(3, -1)
    evaluated = evaluate(coef_table, points).reshape(components, gz_count, items, block_points)
    returned = lax.all_to_all(
        as_sent(jnp.moveaxis(evaluated, 0, 2)), "gz", split_axis=0, concat_axis=0, tiled=True
    )
    source = returned[patch_ids, slot_rank]
    spread = jnp.moveaxis(source, 1, 0).reshape(components, -1)
    right_side = (
        right_side.reshape(components, -1)
        .at[:, cell_ids.reshape(-1)]
        .add(spread)
        .reshape(right_side.shape)
    )
    section_h = field_h + HALF_STEP * field_p
    section_p = field_p + HALF_STEP * right_side
    flat_field = padded.reshape(components, -1)
    point_values = trilinear(
        flat_field, height_cells + 4, width_cells + 4, sph_cells, sph_frac
    ).astype(jnp.bfloat16)
    sphere_of = sph_points // NANG
    angle_of = sph_points % NANG
    share_rows = NSPH // lax.axis_size("gz")
    local_rows = jnp.take(harmonic_table(LMAX, NTHETA, NPHI), angle_of, axis=0)
    spheres_here = jnp.arange(share_rows * lax.axis_size("gz"), dtype=jnp.int32)
    member = (sphere_of[None, :] == spheres_here[:, None]).astype(jnp.bfloat16)
    weighted = (member[:, None, :] * point_values[None]).reshape(
        share_rows * lax.axis_size("gz") * components, -1
    )
    partial_value = sum_at_owner(
        jnp.dot(weighted, local_rows, preferred_element_type=jnp.float32).reshape(
            share_rows * lax.axis_size("gz"), components, -1
        ),
        "gz",
        0,
    )
    mode_out = taken_together(partial_value, ("gx", "gy"))
    return (section_h, section_p, mode_out)


def solution(mesh):
    placed = (
        P(None, "gz", "gy", "gx"),
        P(None, "gz", "gy", "gx"),
        P("gz", "gy", "gx"),
        P(),
        P("gz", "gy", "gx", None, None),
        P("gz", "gy", "gx", None, None, None),
        P("gz", "gy", "gx", None, None),
        P("gz", None, None, None),
        P(("gx", "gy", "gz")),
        P(None, ("gx", "gy", "gz")),
        P(None, ("gx", "gy", "gz")),
    )
    return jax.shard_map(
        shards,
        mesh=mesh,
        in_specs=placed,
        out_specs=(P(None, "gz", "gy", "gx"), P(None, "gz", "gy", "gx"), P("gz", None, None)),
        check_vma=False,
    )
```

profile of v0, /device:TPU:1, one launch (start us, length us, event | category | flops | bytes accessed | tf_op | source)
XLA Modules:
  0.0 191.6 jit_solution(7035828588106324164)
XLA Ops:
  0.7 1.8 copy_dynamic-update-slice_fusion
  2.6 3.9 %collective-permute-start = (f32[10,4,8,2]{3,0,2,1:T(8,128)S(1)}, f32[10,4,8,2]{3,0,2,1:T(8,128)S(1)}, u32[]{:S(2)}, u32[]{:S(2)}) collective-permute-start(f32[10,4,8,2]{3,0,2,1:T(8,128)S(1)} %get-tuple-element.43), channel_id=1, source_target_pairs={{0,128},{128,256},{256,384},{1,129},{129,257},{257,385},{2,130},{1... | collective-permute-start | bytes 7688 | tf_op jit(solution)/shard_map/ppermute | solution.py:22
  6.5 1.3 collective-permute-start.1
  11.6 15.7 %all-to-all-start = ((bf16[32,2,3,128]{3,1,2,0:T(2,128)(2,1)}), bf16[32,2,3,128]{3,1,2,0:T(2,128)(2,1)S(1)}, u32[]{:S(2)}, u32[]{:S(2)}) async-start(bf16[32,2,3,128]{3,1,2,0:T(2,128)(2,1)} %copy.192), calls=%async_computation | async-start | bytes 98304 | tf_op jit(solution)/shard_map/all_to_all | solution.py:203
  34.5 3.4 %collective-permute-start.2 = (f32[10,4,2,132]{3,0,2,1:T(8,128)S(1)}, f32[10,4,2,132]{3,0,2,1:T(8,128)S(1)}, u32[]{:S(2)}, u32[]{:S(2)}) collective-permute-start(f32[10,4,2,132]{3,0,2,1:T(8,128)S(1)} %get-tuple-element.41), channel_id=1, source_target_pairs={{0,32},{32,64},{64,96},{1,33},{33,65},{65,97},{2,34},{34,66},{66,9... | collective-permute-start | bytes 126728 | tf_op jit(solution)/shard_map/ppermute | solution.py:22
  37.9 1.9 %collective-permute-start.3 = (f32[10,4,2,132]{3,0,2,1:T(8,128)S(1)}, f32[10,4,2,132]{3,0,2,1:T(8,128)S(1)}, u32[]{:S(2)}, u32[]{:S(2)}) collective-permute-start(f32[10,4,2,132]{3,0,2,1:T(8,128)S(1)} %get-tuple-element.40), channel_id=1, source_target_pairs={{32,0},{64,32},{96,64},{33,1},{65,33},{97,65},{34,2},{66,34},{98,6... | collective-permute-start | bytes 126728 | tf_op jit(solution)/shard_map/ppermute | solution.py:25
  39.9 3.8 %gather_fusion.1 = bf16[128,961]{1,0:T(8,128)(2,1)S(1)} fusion(bf16[2048,961]{1,0:T(8,128)(2,1)} %constant.100, s32[1024]{0:T(1024)S(1)} %get-tuple-element.72), kind=kCustom, calls=%fused_computation.9 | custom fusion | bytes 492544 | tf_op jit(solution)/shard_map/jit(_take)/gather | solution.py:229
  44.6 3.4 %collective-permute-start.5 = (f32[10,2,12,132]{3,0,2,1:T(8,128)S(1)}, f32[10,2,12,132]{3,0,2,1:T(8,128)S(1)}, u32[]{:S(2)}, u32[]{:S(2)}) collective-permute-start(f32[10,2,12,132]{3,0,2,1:T(8,128)S(1)} %get-tuple-element.39), channel_id=1, source_target_pairs={{0,1},{1,2},{2,3},{3,4},{4,5},{5,6},{6,7},{7,8},{8,9},{9,10},{10,1... | collective-permute-start | bytes 380168 | tf_op jit(solution)/shard_map/ppermute | solution.py:22
  48.0 1.3 collective-permute-start.4
  51.3 1.8 stack.6
  53.1 1.8 stack.8
  56.0 4.8 %fusion.3 = bf16[8192,10]{0,1:T(8,128)(2,1)} fusion(f32[8192,8]{0,1:T(8,128)} %bitcast.178, f32[8,8192]{1,0:T(8,128)} %stack.8, f32[8,8192]{1,0:T(8,128)} %stack.7, f32[1,10,8,64]{3,2,1,0:T(8,128)S(1)} %copy-done), kind=kOutput, calls=%fused_computation.17 | convolution fusion | flops 505069568 | bytes 970752 | tf_op jit(solution)/shard_map/dot_general | solution.py:115
  62.6 13.9 %all-to-all-start.1 = ((bf16[32,2,10,128]{3,1,2,0:T(2,128)(2,1)}), bf16[32,2,10,128]{3,1,2,0:T(2,128)(2,1)S(1)}, u32[]{:S(2)}, u32[]{:S(2)}) async-start(bf16[32,2,10,128]{3,1,2,0:T(2,128)(2,1)} %copy.193), calls=%async_computation.1 | async-start | bytes 327680 | tf_op jit(solution)/shard_map/all_to_all | solution.py:209
  79.4 4.1 %copy.200 = f32[10,12672]{0,1:T(8,128)} copy(f32[10,12672]{1,0:T(8,128)S(1)} %reshape.494) | data formatting | bytes 1013760 | tf_op jit(solution)/shard_map/reshape | solution.py:222
  83.6 3.6 %gather_fusion.9 = f32[128,10]{1,0:T(8,128)S(1)} fusion(f32[10,12672]{0,1:T(8,128)} %copy.200, s32[1024]{0:T(1024)} %get-tuple-element.73), kind=kCustom, calls=%fused_computation.7.clone | custom fusion | bytes 10752 | tf_op jit(solution)/shard_map/jit(_take)/gather | solution.py:161
  87.2 3.6 %gather_fusion.8 = f32[128,10]{1,0:T(8,128)S(1)} fusion(f32[10,12672]{0,1:T(8,128)} %copy.200, s32[1024]{0:T(1024)} %get-tuple-element.74), kind=kCustom, calls=%fused_computation.6.clone | custom fusion | bytes 10752 | tf_op jit(solution)/shard_map/jit(_take)/gather | solution.py:161
  90.9 3.6 %gather_fusion.7 = f32[128,10]{1,0:T(8,128)S(1)} fusion(f32[10,12672]{0,1:T(8,128)} %copy.200, s32[1024]{0:T(1024)} %get-tuple-element.75), kind=kCustom, calls=%fused_computation.5.clone | custom fusion | bytes 10752 | tf_op jit(solution)/shard_map/jit(_take)/gather | solution.py:161
  94.6 3.6 %gather_fusion.6 = f32[128,10]{1,0:T(8,128)S(1)} fusion(f32[10,12672]{0,1:T(8,128)} %copy.200, s32[1024]{0:T(1024)} %get-tuple-element.76), kind=kCustom, calls=%fused_computation.4.clone | custom fusion | bytes 10752 | tf_op jit(solution)/shard_map/jit(_take)/gather | solution.py:161
  98.3 3.6 %gather_fusion.5 = f32[128,10]{1,0:T(8,128)S(1)} fusion(f32[10,12672]{0,1:T(8,128)} %copy.200, s32[1024]{0:T(1024)} %get-tuple-element.77), kind=kCustom, calls=%fused_computation.3.clone | custom fusion | bytes 10752 | tf_op jit(solution)/shard_map/jit(_take)/gather | solution.py:161
  102.0 3.6 %gather_fusion.4 = f32[128,10]{1,0:T(8,128)S(1)} fusion(f32[10,12672]{0,1:T(8,128)} %copy.200, s32[1024]{0:T(1024)} %get-tuple-element.78), kind=kCustom, calls=%fused_computation.2.clone | custom fusion | bytes 10752 | tf_op jit(solution)/shard_map/jit(_take)/gather | solution.py:161
  105.7 3.6 %gather_fusion.3 = f32[128,10]{1,0:T(8,128)S(1)} fusion(f32[10,12672]{0,1:T(8,128)} %copy.200, s32[1024]{0:T(1024)} %get-tuple-element.79), kind=kCustom, calls=%fused_computation.1.clone | custom fusion | bytes 10752 | tf_op jit(solution)/shard_map/jit(_take)/gather | solution.py:161
  109.4 3.5 %gather_fusion.2 = f32[128,10]{1,0:T(8,128)S(1)} fusion(f32[10,12672]{0,1:T(8,128)} %copy.200, s32[1024]{0:T(1024)S(1)} %pad_clamp_fusion.8), kind=kCustom, calls=%fused_computation.clone | custom fusion | bytes 10752 | tf_op jit(solution)/shard_map/jit(_take)/gather | solution.py:161
  113.6 2.4 %copy.217 = f32[32,1,10,961]{3,1,2,0:T(1,128)} copy(f32[32,1,10,961]{3,0,2,1:T(8,128)S(1)} %convolution_bitcast_fusion.1) | data formatting | bytes 2460160 | tf_op jit(solution)/shard_map/dot_general | solution.py:236
  116.0 11.7 %all-to-all-start.2 = ((f32[32,1,10,961]{3,1,2,0:T(1,128)}), f32[32,1,10,961]{3,1,2,0:T(1,128)}, u32[]{:S(2)}, u32[]{:S(2)}) async-start(f32[32,1,10,961]{3,1,2,0:T(1,128)} %copy.217), calls=%async_computation.2 | async-start | bytes 2621440 | tf_op jit(solution)/shard_map/all_to_all | solution.py:42
  130.4 6.8 %scatter_fusion.1 = f32[10,4096]{0,1:T(8,128)S(1)} fusion(f32[10,4096]{0,1:T(8,128)S(1)} %bitcast.165, s32[1024]{0:T(1024)S(1)} %bitcast.182, f32[1024,10]{1,0:T(8,128)S(1)} %copy.197), kind=kCustom, calls=%fused_computation.11 | custom fusion | flops 10240 | bytes 126976 | tf_op jit(solution)/shard_map/scatter-add | solution.py:217
  137.2 33.1 %all-to-all-done.2 = f32[32,1,10,961]{3,1,2,0:T(1,128)} async-done(((f32[32,1,10,961]{3,1,2,0:T(1,128)}), f32[32,1,10,961]{3,1,2,0:T(1,128)}, u32[]{:S(2)}, u32[]{:S(2)}) %all-to-all-start.2) | async-done | bytes 1230112 | tf_op jit(solution)/shard_map/all_to_all | solution.py:42
  170.4 2.1 %reduce_sum.33 = f32[10,961]{1,0:T(8,128)S(1)} reduce(f32[32,1,10,961]{3,1,2,0:T(1,128)} %all-to-all-done.2, f32[]{:T(128)} %constant.76.clone.1), dimensions={0,1}, to_apply=%region_3.0 | reduce | flops 297910 | bytes 1268524 | tf_op jit(solution)/shard_map/reduce_sum | solution.py:43
  172.5 1.2 broadcast_in_dim.26
  173.7 5.7 %all-to-all-start.3 = ((f32[16,1,10,961]{3,1,2,0:T(1,128)}), f32[16,1,10,961]{3,1,2,0:T(1,128)S(1)}, u32[]{:S(2)}, u32[]{:S(2)}) async-start(f32[16,1,10,961]{3,1,2,0:T(1,128)} %broadcast_in_dim.26), calls=%async_computation.3 | async-start | bytes 1310720 | tf_op jit(solution)/shard_map/all_to_all | solution.py:48
  179.4 1.5 broadcast_multiply_fusion
  180.9 2.3 %copy.198 = f32[10,4,8,128]{3,2,1,0:T(8,128)S(1)} copy(f32[10,4,8,128]{0,3,2,1:T(8,128)} %bitcast.166) | data formatting | bytes 327680 | tf_op jit(solution)/shard_map/mul | solution.py:221
  183.9 6.6 %all-to-all-done.3 = f32[16,1,10,961]{3,1,2,0:T(1,128)S(1)} async-done(((f32[16,1,10,961]{3,1,2,0:T(1,128)}), f32[16,1,10,961]{3,1,2,0:T(1,128)S(1)}, u32[]{:S(2)}, u32[]{:S(2)}) %all-to-all-start.3) | async-done | bytes 615072 | tf_op jit(solution)/shard_map/all_to_all | solution.py:48
  (141 shorter events, 24.9 us)
Async XLA Ops:
  0.6 55.4 %copy-start = (f32[1,10,8,64]{3,2,1,0:T(8,128)S(1)}, f32[1,10,8,64]{3,2,1,0:T(8,128)}, u32[]{:S(2)}) copy-start(f32[1,10,8,64]{3,2,1,0:T(8,128)} %param.21) | copy-start | bytes 61444
  0.6 26.7 %copy-start.10 = (s32[3,128]{1,0:T(4,128)S(1)}, s32[3,128]{1,0:T(4,128)}, u32[]{:S(2)}) copy-start(s32[3,128]{1,0:T(4,128)} %param.23) | copy-start | bytes 4612
  0.7 29.5 %copy-start.11 = (f32[3,128]{1,0:T(4,128)S(1)}, f32[3,128]{1,0:T(4,128)}, u32[]{:S(2)}) copy-start(f32[3,128]{1,0:T(4,128)} %param.24) | copy-start | bytes 4612
  0.7 30.7 %copy-start.32 = (s32[128]{0:T(128)S(1)}, s32[128]{0:T(128)}, u32[]{:S(2)}) copy-start(s32[128]{0:T(128)} %param.22) | copy-start | bytes 1540
  2.6 31.8 %collective-permute-start = (f32[10,4,8,2]{3,0,2,1:T(8,128)S(1)}, f32[10,4,8,2]{3,0,2,1:T(8,128)S(1)}, u32[]{:S(2)}, u32[]{:S(2)}) collective-permute-start(f32[10,4,8,2]{3,0,2,1:T(8,128)S(1)} %get-tuple-element.43), channel_id=1, source_target_pairs={{0,128},{128,256},{256,384},{1,129},{129,257},{257,385},{2,130},{1... | collective-permute-start | bytes 7688 | tf_op jit(solution)/shard_map/ppermute | solution.py:22
  6.5 27.8 %collective-permute-start.1 = (f32[10,4,8,2]{3,0,2,1:T(8,128)S(1)}, f32[10,4,8,2]{3,0,2,1:T(8,128)S(1)}, u32[]{:S(2)}, u32[]{:S(2)}) collective-permute-start(f32[10,4,8,2]{3,0,2,1:T(8,128)S(1)} %get-tuple-element.42), channel_id=1, source_target_pairs={{128,0},{256,128},{384,256},{129,1},{257,129},{385,257},{130,2},{2... | collective-permute-start | bytes 7688 | tf_op jit(solution)/shard_map/ppermute | solution.py:25
  11.6 37.7 %all-to-all-start = ((bf16[32,2,3,128]{3,1,2,0:T(2,128)(2,1)}), bf16[32,2,3,128]{3,1,2,0:T(2,128)(2,1)S(1)}, u32[]{:S(2)}, u32[]{:S(2)}) async-start(bf16[32,2,3,128]{3,1,2,0:T(2,128)(2,1)} %copy.192), calls=%async_computation | async-start | bytes 98304 | tf_op jit(solution)/shard_map/all_to_all | solution.py:203
  34.5 9.2 %collective-permute-start.2 = (f32[10,4,2,132]{3,0,2,1:T(8,128)S(1)}, f32[10,4,2,132]{3,0,2,1:T(8,128)S(1)}, u32[]{:S(2)}, u32[]{:S(2)}) collective-permute-start(f32[10,4,2,132]{3,0,2,1:T(8,128)S(1)} %get-tuple-element.41), channel_id=1, source_target_pairs={{0,32},{32,64},{64,96},{1,33},{33,65},{65,97},{2,34},{34,66},{66,9... | collective-permute-start | bytes 126728 | tf_op jit(solution)/shard_map/ppermute | solution.py:22
  37.9 6.3 %collective-permute-start.3 = (f32[10,4,2,132]{3,0,2,1:T(8,128)S(1)}, f32[10,4,2,132]{3,0,2,1:T(8,128)S(1)}, u32[]{:S(2)}, u32[]{:S(2)}) collective-permute-start(f32[10,4,2,132]{3,0,2,1:T(8,128)S(1)} %get-tuple-element.40), channel_id=1, source_target_pairs={{32,0},{64,32},{96,64},{33,1},{65,33},{97,65},{34,2},{66,34},{98,6... | collective-permute-start | bytes 126728 | tf_op jit(solution)/shard_map/ppermute | solution.py:25
  44.2 32.3 %copy-start.2 = (f32[10,4,2,132]{3,0,2,1:T(8,128)}, f32[10,4,2,132]{3,0,2,1:T(8,128)S(1)}, u32[]{:S(2)}) copy-start(f32[10,4,2,132]{3,0,2,1:T(8,128)S(1)} %collective-permute-done.3) | copy-start | bytes 126724
  44.6 31.9 %collective-permute-start.5 = (f32[10,2,12,132]{3,0,2,1:T(8,128)S(1)}, f32[10,2,12,132]{3,0,2,1:T(8,128)S(1)}, u32[]{:S(2)}, u32[]{:S(2)}) collective-permute-start(f32[10,2,12,132]{3,0,2,1:T(8,128)S(1)} %get-tuple-element.39), channel_id=1, source_target_pairs={{0,1},{1,2},{2,3},{3,4},{4,5},{5,6},{6,7},{7,8},{8,9},{9,10},{10,1... | collective-permute-start | bytes 380168 | tf_op jit(solution)/shard_map/ppermute | solution.py:22
  48.0 28.5 %collective-permute-start.4 = (f32[10,2,12,132]{3,0,2,1:T(8,128)S(1)}, f32[10,2,12,132]{3,0,2,1:T(8,128)S(1)}, u32[]{:S(2)}, u32[]{:S(2)}) collective-permute-start(f32[10,2,12,132]{3,0,2,1:T(8,128)S(1)} %get-tuple-element.38), channel_id=1, source_target_pairs={{1,0},{2,1},{3,2},{4,3},{5,4},{6,5},{7,6},{8,7},{9,8},{10,9},{11,1... | collective-permute-start | bytes 380168 | tf_op jit(solution)/shard_map/ppermute | solution.py:25
  62.6 53.4 %all-to-all-start.1 = ((bf16[32,2,10,128]{3,1,2,0:T(2,128)(2,1)}), bf16[32,2,10,128]{3,1,2,0:T(2,128)(2,1)S(1)}, u32[]{:S(2)}, u32[]{:S(2)}) async-start(bf16[32,2,10,128]{3,1,2,0:T(2,128)(2,1)} %copy.193), calls=%async_computation.1 | async-start | bytes 327680 | tf_op jit(solution)/shard_map/all_to_all | solution.py:209
  79.3 33.7 %copy-start.13 = (f32[128]{0:T(128)S(1)}, f32[128]{0:T(128)}, u32[]{:S(2)}) copy-start(f32[128]{0:T(128)} %get-tuple-element.61) | copy-start | bytes 1540
  79.3 33.7 %copy-start.14 = (f32[128]{0:T(128)S(1)}, f32[128]{0:T(128)}, u32[]{:S(2)}) copy-start(f32[128]{0:T(128)} %get-tuple-element.62) | copy-start | bytes 1540
  79.3 33.7 %copy-start.15 = (f32[128]{0:T(128)S(1)}, f32[128]{0:T(128)}, u32[]{:S(2)}) copy-start(f32[128]{0:T(128)} %get-tuple-element.63) | copy-start | bytes 1540
  79.3 33.7 %copy-start.16 = (f32[128]{0:T(128)S(1)}, f32[128]{0:T(128)}, u32[]{:S(2)}) copy-start(f32[128]{0:T(128)} %get-tuple-element.64) | copy-start | bytes 1540
  79.3 33.7 %copy-start.17 = (f32[128]{0:T(128)S(1)}, f32[128]{0:T(128)}, u32[]{:S(2)}) copy-start(f32[128]{0:T(128)} %get-tuple-element.65) | copy-start | bytes 1540
  79.3 33.7 %copy-start.18 = (f32[128]{0:T(128)S(1)}, f32[128]{0:T(128)}, u32[]{:S(2)}) copy-start(f32[128]{0:T(128)} %get-tuple-element.66) | copy-start | bytes 1540
  79.3 33.7 %copy-start.19 = (f32[128]{0:T(128)S(1)}, f32[128]{0:T(128)}, u32[]{:S(2)}) copy-start(f32[128]{0:T(128)} %get-tuple-element.67) | copy-start | bytes 1540
  79.3 33.7 %copy-start.20 = (f32[128]{0:T(128)S(1)}, f32[128]{0:T(128)}, u32[]{:S(2)}) copy-start(f32[128]{0:T(128)} %get-tuple-element.68) | copy-start | bytes 1540
  79.4 33.7 %copy-start.21 = (pred[128]{0:T(512)(128)(4,1)S(1)}, pred[128]{0:T(512)(128)(4,1)}, u32[]{:S(2)}) copy-start(pred[128]{0:T(512)(128)(4,1)} %get-tuple-element.4) | copy-start | bytes 388
  79.4 33.7 %copy-start.22 = (pred[128]{0:T(512)(128)(4,1)S(1)}, pred[128]{0:T(512)(128)(4,1)}, u32[]{:S(2)}) copy-start(pred[128]{0:T(512)(128)(4,1)} %get-tuple-element.16) | copy-start | bytes 388
  79.4 33.7 %copy-start.23 = (pred[128]{0:T(512)(128)(4,1)S(1)}, pred[128]{0:T(512)(128)(4,1)}, u32[]{:S(2)}) copy-start(pred[128]{0:T(512)(128)(4,1)} %get-tuple-element.59) | copy-start | bytes 388
  79.4 33.7 %copy-start.24 = (pred[128]{0:T(512)(128)(4,1)S(1)}, pred[128]{0:T(512)(128)(4,1)}, u32[]{:S(2)}) copy-start(pred[128]{0:T(512)(128)(4,1)} %get-tuple-element.7) | copy-start | bytes 388
  79.4 33.7 %copy-start.25 = (pred[128]{0:T(512)(128)(4,1)S(1)}, pred[128]{0:T(512)(128)(4,1)}, u32[]{:S(2)}) copy-start(pred[128]{0:T(512)(128)(4,1)} %get-tuple-element.57) | copy-start | bytes 388
  79.4 33.7 %copy-start.26 = (pred[128]{0:T(512)(128)(4,1)S(1)}, pred[128]{0:T(512)(128)(4,1)}, u32[]{:S(2)}) copy-start(pred[128]{0:T(512)(128)(4,1)} %get-tuple-element.69) | copy-start | bytes 388
  79.4 33.7 %copy-start.27 = (pred[128]{0:T(512)(128)(4,1)S(1)}, pred[128]{0:T(512)(128)(4,1)}, u32[]{:S(2)}) copy-start(pred[128]{0:T(512)(128)(4,1)} %get-tuple-element.20) | copy-start | bytes 388
  79.4 33.7 %copy-start.29 = (pred[128]{0:T(512)(128)(4,1)S(1)}, pred[128]{0:T(512)(128)(4,1)}, u32[]{:S(2)}) copy-start(pred[128]{0:T(512)(128)(4,1)} %get-tuple-element.11) | copy-start | bytes 388
  79.4 33.7 %copy-start.28 = (pred[128]{0:T(512)(128)(4,1)S(1)}, pred[128]{0:T(512)(128)(4,1)}, u32[]{:S(2)}) copy-start(pred[128]{0:T(512)(128)(4,1)} %get-tuple-element.22) | copy-start | bytes 388
  116.0 54.4 %all-to-all-start.2 = ((f32[32,1,10,961]{3,1,2,0:T(1,128)}), f32[32,1,10,961]{3,1,2,0:T(1,128)}, u32[]{:S(2)}, u32[]{:S(2)}) async-start(f32[32,1,10,961]{3,1,2,0:T(1,128)} %copy.217), calls=%async_computation.2 | async-start | bytes 2621440 | tf_op jit(solution)/shard_map/all_to_all | solution.py:42
  173.7 16.8 %all-to-all-start.3 = ((f32[16,1,10,961]{3,1,2,0:T(1,128)}), f32[16,1,10,961]{3,1,2,0:T(1,128)S(1)}, u32[]{:S(2)}, u32[]{:S(2)}) async-start(f32[16,1,10,961]{3,1,2,0:T(1,128)} %broadcast_in_dim.26), calls=%async_computation.3 | async-start | bytes 1310720 | tf_op jit(solution)/shard_map/all_to_all | solution.py:48
  (11 other events, 93.6 us)
where the time goes:
time: 195 us; the launch traced here: 192 us
  starting transfers between devices  62.3 us (32%)
  local copies, waits for them, and re-layouts  58.6 us (30%)
  waiting for transfers between devices  40.3 us (21%)
  other arithmetic  22.8 us (12%)
  matrix products  6.21 us (3%)
    all_to_all x1, waiting for transfers between devices, sum_at_owner(): lax.all_to_all(tiles, axis, split_axis=0, concat_axis=0, tiled=True)  33.1 us
    gather x16, local copies, waits for them, and re-layouts, trilinear(): jnp.take(flat_field, position, axis=1)  29.4 us
    all_to_all x1, starting transfers between devices, shards(): lax.all_to_all(outbox.astype(jnp.bfloat16), 'gz', split_axis=0, concat_ax...  15.7 us
    all_to_all x1, starting transfers between devices, shards(): lax.all_to_all(as_sent(jnp.moveaxis(evaluated, 0, 2)), 'gz', split_axis=0...  13.9 us
    all_to_all x1, starting transfers between devices, sum_at_owner(): lax.all_to_all(tiles, axis, split_axis=0, concat_axis=0, tiled=True)  11.7 us
    ppermute x3, starting transfers between devices, with_halo(): lax.ppermute(lax.slice_in_dim(block, block.shape[dim] - width, None, axis...  10.8 us
    scatter-add x1, other arithmetic, shards(): right_side = right_side.reshape(components, -1).at[:, cell_ids.reshape(-1...  6.8 us
    all_to_all x1, waiting for transfers between devices, sent_to_all(): lax.all_to_all(jnp.broadcast_to(value[None], (size, *value.shape)), axis,...  6.58 us
  transfers between devices with their start and end apart: 10, of which 3 were waited for; matrix products, arithmetic and copies ran while one was open for 42% of the time, Pallas kernels for 0%

commit v1 on v0

v1 whole, which is shorter than its diff:
```python
import functools

import jax
import jax.numpy as jnp
import numpy as np
from jax import lax
from jax.experimental import pallas as pl
from jax.experimental.pallas import tpu as pltpu
from jax.sharding import PartitionSpec as P

LMAX = 30
NTHETA = 32
NPHI = 64
NANG = NTHETA * NPHI
NMODE = (LMAX + 1) ** 2
HALF_STEP = 0.125

COMP = 10
CZ = 4
CY = 8
CX = 128
LANES = 128
ROWS_OWN = COMP * CZ * CY
ROWS_SLAB = COMP * 2 * CY
ROWS_ALL = ROWS_OWN + 4 * ROWS_SLAB
MODE_TILES = 8
MODE_ROWS = COMP * MODE_TILES
CHEB = 8
COEF_ROWS = COMP * CHEB * CHEB * CHEB // LANES
POINT_ROWS = 16
SLOTS = 8

F32 = jnp.float32
BF16 = jnp.bfloat16
HIGHEST = lax.Precision.HIGHEST
NN = (((1,), (0,)), ((), ()))
NT = (((1,), (1,)), ((), ()))
TN = (((0,), (0,)), ((), ()))


def mode_factors():
    polar = np.pi * (np.arange(NTHETA) + 0.5) / NTHETA
    azimuth = 2.0 * np.pi * np.arange(NPHI) / NPHI
    cosine, sine = np.cos(polar), np.sin(polar)
    legendre = np.zeros((LMAX + 1, LMAX + 1, NTHETA))
    diagonal = np.full(NTHETA, np.sqrt(0.25 / np.pi))
    for m in range(LMAX + 1):
        if m > 0:
            diagonal = diagonal * sine * np.sqrt((2.0 * m + 1.0) / (2.0 * m))
        legendre[m, m] = diagonal
        if m < LMAX:
            legendre[m + 1, m] = cosine * np.sqrt(2.0 * m + 3.0) * diagonal
        for l in range(m + 2, LMAX + 1):
            a = np.sqrt((4.0 * l * l - 1.0) / (l * l - m * m))
            b = np.sqrt(((l - 1.0) ** 2 - m * m) / (4.0 * (l - 1.0) ** 2 - 1.0))
            legendre[l, m] = a * (cosine * legendre[l - 1, m] - b * legendre[l - 2, m])
    width = MODE_TILES * LANES
    radial = np.zeros((NTHETA, width))
    angular = np.zeros((NPHI, width))
    weight = sine * np.pi / NTHETA
    for l in range(LMAX + 1):
        for m in range(-l, l + 1):
            n = l * l + l + m
            radial[:, n] = legendre[l, abs(m)] * weight
            if m == 0:
                angular[:, n] = 1.0
            elif m > 0:
                angular[:, n] = np.sqrt(2.0) * np.cos(m * azimuth)
            else:
                angular[:, n] = np.sqrt(2.0) * np.sin(-m * azimuth)
    angular = angular.astype(np.float32)
    high = angular.astype(jnp.bfloat16)
    low = (angular - high.astype(np.float32)).astype(jnp.bfloat16)
    return radial.astype(np.float32), np.concatenate([high, low], axis=0)


def iota(shape, dim):
    return lax.broadcasted_iota(jnp.int32, shape, dim)


def split2(value):
    high = value.astype(BF16)
    return high, (value - high.astype(F32)).astype(BF16)


def dot(a, b, dims, precision=None):
    return lax.dot_general(a, b, dims, precision=precision, preferred_element_type=F32)


def two_hot(position, cell, fraction):
    return jnp.where(position == cell, 1.0 - fraction, 0.0) + jnp.where(
        position == cell + 1, fraction, 0.0
    )


def weighted_rows(parts, cells, frac):
    own, zl, zh, yl, yh = parts
    lane8 = iota((8, LANES), 0)
    row16 = iota((16, LANES), 0)
    wy = two_hot(lane8 + 2, cells[1:2], frac[1:2])
    plane = [two_hot(z, cells[0:1], frac[0:1]) * wy for z in range(CZ + 4)]
    wz16 = two_hot(row16 // 2, cells[0:1], frac[0:1])
    wyl = wz16 * two_hot(row16 % 2, cells[1:2], frac[1:2])
    wyh = wz16 * two_hot(row16 % 2 + CY + 2, cells[1:2], frac[1:2])
    rows = []
    for c in range(COMP):
        total = jnp.zeros((8, LANES), F32)
        for z in range(CZ):
            base = (c * CZ + z) * CY
            total += own[base : base + 8] * plane[z + 2]
        for z in range(2):
            base = (c * 2 + z) * CY
            total += zl[base : base + 8] * plane[z]
            total += zh[base : base + 8] * plane[z + 6]
            base = c * 16 + z * 8
            total += yl[base : base + 8] * wyl[z * 8 : z * 8 + 8]
            total += yh[base : base + 8] * wyh[z * 8 : z * 8 + 8]
        rows.append(jnp.sum(total, axis=0, keepdims=True))
    return jnp.concatenate(rows, axis=0)


def y_slab_kernel(h, zl, zh, first, last):
    for c in range(COMP):
        for z in range(CZ + 4):
            source = zl.at[c, z] if z < 2 else h.at[c, z - 2] if z < CZ + 2 else zh.at[c, z - CZ - 2]
            row = (c * (CZ + 4) + z) * 2
            first[row : row + 2, :] = source[0:2, :]
            last[row : row + 2, :] = source[CY - 2 : CY, :]


def all_rows(h, zl, zh, yl, yh):
    return (
        h[...].reshape(ROWS_OWN, LANES),
        zl[...].reshape(ROWS_SLAB, LANES),
        zh[...].reshape(ROWS_SLAB, LANES),
        yl[...],
        yh[...],
    )


def x_edge_kernel(h, zl, zh, yl, yh, first, last):
    row = iota((8, LANES), 0)
    lane = iota((8, LANES), 1)
    place = jnp.where(row < 2, row, row + CX - 4)
    pick = jnp.where(lane == place, 1.0, 0.0).astype(BF16)
    at = 0
    for part in all_rows(h, zl, zh, yl, yh):
        high, low = split2(part)
        edge = dot(pick, high, NT) + dot(pick, low, NT)
        size = part.shape[0]
        first[:, at : at + size] = edge[0:2]
        last[:, at : at + size] = edge[2:4]
        at += size


def interior_points_kernel(h, zl, zh, yl, yh, cells, frac, out):
    cell, fraction = cells[...], frac[...]
    wx = two_hot(iota((CX, LANES), 0) + 2, cell[2:3], fraction[2:3])
    parts = [dot(part, wx, NN, HIGHEST) for part in all_rows(h, zl, zh, yl, yh)]
    out[...] = weighted_rows(parts, cell, fraction)


def pack_kernel(inner, xl, xr, cells, frac, points, coef, out):
    cell, fraction = cells[...], frac[...]
    edges = jnp.concatenate([xl[...], xr[...]], axis=0)
    place = iota((4, LANES), 0)
    place = jnp.where(place < 2, place, place + CX)
    wx = two_hot(place, cell[2:3], fraction[2:3])
    grown = dot(edges, wx, TN, HIGHEST)
    cuts = (0, 320, 480, 640, 800, 960)
    parts = [grown[a:b] for a, b in zip(cuts[:-1], cuts[1:])]
    values = inner[...] + weighted_rows(parts, cell, fraction)
    point = points[...]
    sphere = point // NANG
    polar = (point // NPHI % NTHETA).astype(F32)
    azimuth = (point % NPHI).astype(F32)
    tail = jnp.zeros((POINT_ROWS - COMP - 2, LANES), F32)
    coefficients = coef[...].astype(BF16)
    for s in range(out.shape[0]):
        node = jnp.where(sphere == s, polar, 255.0)
        block = jnp.concatenate([values, node, azimuth, tail], axis=0)
        out[s, 0:POINT_ROWS, :] = block.astype(BF16)
        out[s, POINT_ROWS : POINT_ROWS + COEF_ROWS, :] = coefficients


def partial_modes_kernel(arrived, radial, angular, out, rows):
    row_i = iota((NTHETA, LANES), 0).astype(F32)
    row_j = iota((NPHI, LANES), 0).astype(F32)
    dense = jnp.zeros((COMP * NTHETA, NPHI), F32)
    for s in range(0, arrived.shape[0], 2):
        left, right = [], []
        for k in (s, s + 1):
            block = arrived[k, 0:POINT_ROWS, :].astype(F32)
            at_i = row_i == block[COMP : COMP + 1]
            at_j = row_j == block[COMP + 1 : COMP + 2]
            left.append(
                jnp.concatenate(
                    [jnp.where(at_i, block[c : c + 1], 0.0) for c in range(COMP)], axis=0
                ).astype(BF16)
            )
            right.append(jnp.where(at_j, 1.0, 0.0).astype(BF16))
        dense += dot(
            jnp.concatenate(left, axis=1), jnp.concatenate(right, axis=1), NT
        )
    exact = dense.astype(BF16)
    exact = jnp.concatenate([exact, exact], axis=1)
    for t in range(MODE_TILES):
        lanes = slice(t * LANES, (t + 1) * LANES)
        grown = dot(exact, angular[:, lanes], NN)
        weight = radial[:, lanes]
        for c in range(COMP):
            part = grown[c * NTHETA : (c + 1) * NTHETA] * weight
            rows[t * COMP + c : t * COMP + c + 1, :] = jnp.sum(part, axis=0, keepdims=True)
    sent = rows[...].astype(BF16)
    for k in range(out.shape[0]):
        out[k] = sent


def sum_modes_kernel(arrived, out):
    total = arrived[0].astype(F32)
    for k in range(1, arrived.shape[0]):
        total += arrived[k].astype(F32)
    for t in range(MODE_TILES):
        width = min(LANES, NMODE - t * LANES)
        for c in range(COMP):
            row = t * COMP + c
            out[c, :, t * LANES : t * LANES + width] = total[row : row + 1, :width]


def right_side_kernel(h, zl, zh, yl, yh, p, potential, coupling, section_h, out):
    row = iota((CY, LANES), 0)
    lane = iota((CY, LANES), 1)
    for c in range(COMP):
        layers = [zl[c, 0], zl[c, 1]] + [h[c, z] for z in range(CZ)] + [zh[c, 0], zh[c, 1]]
        for z in range(CZ):
            mid = layers[z + 2]
            along_z = 16.0 * (layers[z + 1] + layers[z + 3]) - (layers[z] + layers[z + 4])
            at = (c * (CZ + 4) + z + 2) * 2
            above, below = yh[at : at + 2, :], yl[at : at + 2, :]
            ring = jnp.concatenate([above, mid[2:6], below], axis=0)
            y1 = pltpu.roll(jnp.where(row == 0, ring, mid), CY - 1, 0)
            y2 = pltpu.roll(jnp.where(row < 2, ring, mid), CY - 2, 0)
            m1 = pltpu.roll(jnp.where(row == CY - 1, ring, mid), 1, 0)
            m2 = pltpu.roll(jnp.where(row >= CY - 2, ring, mid), 2, 0)
            along_y = 16.0 * (y1 + m1) - (y2 + m2)
            x1 = jnp.where(lane < CX - 1, pltpu.roll(mid, CX - 1, 1), 0.0)
            x2 = jnp.where(lane < CX - 2, pltpu.roll(mid, CX - 2, 1), 0.0)
            n1 = jnp.where(lane >= 1, pltpu.roll(mid, 1, 1), 0.0)
            n2 = jnp.where(lane >= 2, pltpu.roll(mid, 2, 1), 0.0)
            along_x = 16.0 * (x1 + n1) - (x2 + n2)
            laplacian = (along_z + along_y + along_x - 90.0 * mid) * (1.0 / 12.0)
            coupled = coupling[c, 0] * h[0, z]
            for b in range(1, COMP):
                coupled += coupling[c, b] * h[b, z]
            momentum = p[c, z]
            section_h[c, z] = mid + HALF_STEP * momentum
            out[c, z] = momentum + HALF_STEP * (laplacian - potential[z] * coupled)


def source_kernel(patch, arrived, coords, cells, partial, xl, xr, out, series, terms, sources):
    for axis in range(3):
        value = coords[axis]
        older, newer = jnp.ones_like(value), value
        for n in range(CHEB):
            series[axis, n * SLOTS : (n + 1) * SLOTS, :] = older
            older, newer = newer, 2.0 * value * newer - older
    for slot in range(SLOTS):
        third = series[2, pl.ds(slot, CHEB, stride=SLOTS), :]
        product = jnp.concatenate(
            [series[1, n * SLOTS + slot : n * SLOTS + slot + 1, :] * third for n in range(CHEB)],
            axis=0,
        )
        high, low = split2(product)
        empty = jnp.zeros((CHEB * CHEB, LANES), BF16)
        block = arrived[patch[slot], POINT_ROWS : POINT_ROWS + COEF_ROWS, :]
        grown = jnp.zeros((COEF_ROWS, 2 * LANES), F32)
        for part in (high, low):
            wide = jnp.concatenate(
                [jnp.concatenate([part, empty], axis=0), jnp.concatenate([empty, part], axis=0)],
                axis=1,
            )
            grown += dot(block, wide, NN)
        even = series[0, pl.ds(slot, 4, stride=2 * SLOTS), :]
        odd = series[0, pl.ds(slot + SLOTS, 4, stride=2 * SLOTS), :]
        even = jnp.concatenate([even] * COMP, axis=0)
        odd = jnp.concatenate([odd] * COMP, axis=0)
        terms[slot * COEF_ROWS : (slot + 1) * COEF_ROWS, :] = (
            grown[:, :LANES] * even + grown[:, LANES:] * odd
        )
    count = SLOTS * COMP
    total = terms[pl.ds(0, count, stride=4), :]
    for m in range(1, 4):
        total += terms[pl.ds(m, count, stride=4), :]
    sources[...] = total
    cell = cells[...]
    layer, column = cell // CX, cell % CX
    row_l = iota((CZ * CY, LANES), 0)
    row_x = iota((CX, LANES), 0)
    added = jnp.zeros((ROWS_OWN, CX), F32)
    for slot in range(0, SLOTS, 2):
        left, right = [], []
        for k in (slot, slot + 1):
            at_l = row_l == layer[k : k + 1]
            at_x = row_x == column[k : k + 1]
            left.append(
                jnp.concatenate(
                    [
                        jnp.where(at_l, sources[k * COMP + c : k * COMP + c + 1, :], 0.0)
                        for c in range(COMP)
                    ],
                    axis=0,
                ).astype(BF16)
            )
            right.append(jnp.where(at_x, 1.0, 0.0).astype(BF16))
        added += dot(jnp.concatenate(left, axis=1), jnp.concatenate(right, axis=1), NT)
    edges = jnp.concatenate([xl[:, :ROWS_OWN], xr[:, :ROWS_OWN]], axis=0)
    place = iota((4, LANES), 0)
    place = jnp.where(place < 2, place - 2, place + CX - 2)
    far = jnp.abs(place - iota((4, LANES), 1))
    stencil = jnp.where(far == 1, 16.0, jnp.where(far == 2, -1.0, 0.0))
    added += dot(edges, stencil, TN, HIGHEST) * (1.0 / 12.0)
    out[...] = partial[...] + HALF_STEP * added.reshape(COMP, CZ, CY, CX)


def call(kernel, outs, scratch=(), smem=(), count=0):
    specs = [
        pl.BlockSpec(memory_space=pltpu.SMEM if k in smem else pltpu.VMEM) for k in range(count)
    ]
    return pl.pallas_call(
        kernel,
        out_shape=outs,
        in_specs=specs,
        scratch_shapes=scratch,
        name=kernel.__name__,
    )


def shape(dims, dtype=F32):
    return jax.ShapeDtypeStruct(dims, dtype)


def neighbours(axis):
    count = lax.axis_size(axis)
    forward = [(i, i + 1) for i in range(count - 1)]
    return forward, [(b, a) for a, b in forward]


def shards(
    field_h,
    field_p,
    potential,
    coupling,
    wt_cells,
    wt_coords,
    wt_patch,
    patch_coef,
    sph_points,
    sph_cells,
    sph_frac,
):
    z_count = lax.axis_size("gz")
    xy_count = lax.axis_size("gx") * lax.axis_size("gy")
    up, down = neighbours("gz")
    zl = lax.ppermute(field_h[:, CZ - 2 :], "gz", up)
    zh = lax.ppermute(field_h[:, :2], "gz", down)
    slab = shape((ROWS_SLAB, LANES))
    first, last = call(y_slab_kernel, (slab, slab), count=3)(field_h, zl, zh)
    up, down = neighbours("gy")
    yl = lax.ppermute(last, "gy", up)
    yh = lax.ppermute(first, "gy", down)
    grid = (field_h, zl, zh, yl, yh)
    edge = shape((2, ROWS_ALL))
    first, last = call(x_edge_kernel, (edge, edge), count=5)(*grid)
    up, down = neighbours("gx")
    xl = lax.ppermute(last, "gx", up)
    xr = lax.ppermute(first, "gx", down)
    inner = call(interior_points_kernel, shape((COMP, LANES)), count=7)(
        *grid, sph_cells, sph_frac
    )
    cube = shape((COMP, CZ, CY, CX))
    section_h, partial = call(right_side_kernel, (cube, cube), count=8, smem=(7,))(
        *grid, field_p, potential, coupling
    )
    packed = call(
        pack_kernel, shape((z_count, POINT_ROWS + COEF_ROWS, LANES), BF16), count=7
    )(
        inner,
        xl,
        xr,
        sph_cells,
        sph_frac,
        sph_points.reshape(1, LANES),
        patch_coef.reshape(COEF_ROWS, LANES),
    )
    arrived = lax.all_to_all(packed, "gz", 0, 0, tiled=True)
    radial, angular = mode_factors()
    sent = call(
        partial_modes_kernel,
        shape((xy_count, MODE_ROWS, LANES), BF16),
        scratch=[pltpu.VMEM((MODE_ROWS, LANES), F32)],
        count=3,
    )(arrived, jnp.asarray(radial), jnp.asarray(angular))
    gathered = lax.all_to_all(sent, ("gx", "gy"), 0, 0, tiled=True)
    section_p = call(
        source_kernel,
        cube,
        scratch=[
            pltpu.VMEM((3, CHEB * SLOTS, LANES), F32),
            pltpu.VMEM((SLOTS * COEF_ROWS, LANES), F32),
            pltpu.VMEM((SLOTS * COMP, LANES), F32),
        ],
        count=7,
        smem=(0,),
    )(
        wt_patch.reshape(SLOTS),
        arrived,
        jnp.moveaxis(wt_coords[0, 0, 0], 1, 0),
        wt_cells[0, 0, 0],
        partial,
        xl,
        xr,
    )
    modes = call(sum_modes_kernel, shape((COMP, 1, NMODE)), count=1)(gathered)
    return section_h, section_p, jnp.moveaxis(modes, 1, 0)


def solution(mesh):
    placed = (
        P(None, "gz", "gy", "gx"),
        P(None, "gz", "gy", "gx"),
        P("gz", "gy", "gx"),
        P(),
        P("gz", "gy", "gx", None, None),
        P("gz", "gy", "gx", None, None, None),
        P("gz", "gy", "gx", None, None),
        P("gz", None, None, None),
        P(("gx", "gy", "gz")),
        P(None, ("gx", "gy", "gz")),
        P(None, ("gx", "gy", "gz")),
    )
    return jax.shard_map(
        shards,
        mesh=mesh,
        in_specs=placed,
        out_specs=(P(None, "gz", "gy", "gx"), P(None, "gz", "gy", "gx"), P("gz", None, None)),
        check_vma=False,
    )
```

time: 195 us -> 93.8 us (0.48); the launches traced: 192 us -> 93.1 us
  local copies, waits for them, and re-layouts: 58.6 us -> 4.23 us
  blocking collectives: 0 us -> 37 us
  starting transfers between devices: 62.3 us -> 27.1 us
  waiting for transfers between devices: 40.3 us -> 5.82 us
  other arithmetic: 22.8 us -> 0 us
  Pallas kernels: 0 us -> 18.1 us
  matrix products: 6.21 us -> 0 us
    all_to_all x4 -> x1, starting transfers between devices: 47 us -> 6.55 us  [shards(): gathered = lax.all_to_all(sent, ('gx', 'gy'), 0, 0, tiled=True)]
    all_to_all x0 -> x1, blocking collectives: none -> 37 us  [shards(): arrived = lax.all_to_all(packed, 'gz', 0, 0, tiled=True)]
    all_to_all x4 -> x1, waiting for transfers between devices: 39.7 us -> 2.93 us  [shards(): gathered = lax.all_to_all(sent, ('gx', 'gy'), 0, 0, tiled=True)]
    gather x18 -> x0, local copies, waits for them, and re-layouts: 33.7 us -> none  [the longest x16 29.4 us: trilinear(): jnp.take(flat_field, position, axis=1)]
    pallas_call x0 -> x8, Pallas kernels: none -> 18.1 us  [the longest x1 3.38 us: shards(): call(partial_modes_kernel, shape((xy_count, MODE_ROWS, LANES), BF16), scr...]
    scatter-add x1 -> x0, other arithmetic: 6.8 us -> none  [shards(): right_side = right_side.reshape(components, -1).at[:, cell_ids.reshape(-1...]
    dot_general x3 -> x0, matrix products: 6.21 us -> none  [the longest x1 4.8 us: evaluate(): jnp.dot(coefficients.reshape(-1, terms * terms), product, precision=lax.P...]
    ppermute x6, starting transfers between devices: 15.3 us -> 20.6 us  [the longest x1 5.45 us: shards(): zl = lax.ppermute(field_h[:, CZ - 2:], 'gz', up)]
  transfers between devices with their start and end apart: 10 -> 7, of which waited for: 3 -> 4; matrix products, arithmetic and copies ran while one was open for 42% -> 1% of each run, Pallas kernels for 0% -> 8%
where the time goes in v1:
time: 93.8 us; the launch traced here: 93.1 us
  blocking collectives  37 us (39%)
  starting transfers between devices  27.1 us (29%)
  Pallas kernels  18.1 us (19%)
  waiting for transfers between devices  5.82 us (6%)
  local copies, waits for them, and re-layouts  4.23 us (5%)
    all_to_all x1, blocking collectives, shards(): arrived = lax.all_to_all(packed, 'gz', 0, 0, tiled=True)  37 us
    all_to_all x1, starting transfers between devices, shards(): gathered = lax.all_to_all(sent, ('gx', 'gy'), 0, 0, tiled=True)  6.55 us
    ppermute x1, starting transfers between devices, shards(): zl = lax.ppermute(field_h[:, CZ - 2:], 'gz', up)  5.45 us
    ppermute x1, starting transfers between devices, shards(): yh = lax.ppermute(first, 'gy', down)  5.1 us
    ppermute x1, starting transfers between devices, shards(): yl = lax.ppermute(last, 'gy', up)  4.61 us
    pallas_call x1, Pallas kernels, shards(): call(partial_modes_kernel, shape((xy_count, MODE_ROWS, LANES), BF16), scr...  3.38 us
    all_to_all x1, waiting for transfers between devices, shards(): gathered = lax.all_to_all(sent, ('gx', 'gy'), 0, 0, tiled=True)  2.93 us
    ppermute x1, starting transfers between devices, shards(): xl = lax.ppermute(last, 'gx', up)  2.85 us
  transfers between devices with their start and end apart: 7, of which 4 were waited for; matrix products, arithmetic and copies ran while one was open for 1% of the time, Pallas kernels for 8%

profile of v1, /device:TPU:1, one launch (start us, length us, event | category | flops | bytes accessed | tf_op | source)
XLA Modules:
  0.0 93.1 jit_solution(12670718428928635531)
XLA Ops:
  0.6 0.9 %fusion = (f32[10,2,8,128]{3,2,1,0:T(8,128)S(1)}, f32[10,2,8,128]{3,2,1,0:T(8,128)S(1)}) fusion(f32[10,4,8,128]{3,2,1,0:T(8,128)} %h.7), kind=kLoop, calls=%fused_computation | loop fusion | bytes 327680 | tf_op jit(solution)/shard_map/slice | solution.py:365
  1.6 1.3 %collective-permute-start.1 = (f32[10,2,8,128]{3,2,1,0:T(8,128)S(1)}, f32[10,2,8,128]{3,2,1,0:T(8,128)S(1)}, u32[]{:S(2)}, u32[]{:S(2)}) collective-permute-start(f32[10,2,8,128]{3,2,1,0:T(8,128)S(1)} %get-tuple-element.15), channel_id=1, source_target_pairs={{1,0},{2,1},{3,2},{4,3},{5,4},{6,5},{7,6},{8,7},{9,8},{10,9},{11,1... | collective-permute-start | bytes 245768 | tf_op jit(solution)/shard_map/ppermute | solution.py:365
  2.9 5.4 %collective-permute-start = (f32[10,2,8,128]{3,2,1,0:T(8,128)S(1)}, f32[10,2,8,128]{3,2,1,0:T(8,128)S(1)}, u32[]{:S(2)}, u32[]{:S(2)}) collective-permute-start(f32[10,2,8,128]{3,2,1,0:T(8,128)S(1)} %get-tuple-element.16), channel_id=1, source_target_pairs={{0,1},{1,2},{2,3},{3,4},{4,5},{5,6},{6,7},{7,8},{8,9},{9,10},{10,1... | collective-permute-start | bytes 245768 | tf_op jit(solution)/shard_map/ppermute | solution.py:364
  8.3 0.0 collective-permute-done.1.zh
  8.3 0.0 copy-start.1
  8.4 1.4 %collective-permute-done.zl = f32[10,2,8,128]{3,2,1,0:T(8,128)S(1)} collective-permute-done((f32[10,2,8,128]{3,2,1,0:T(8,128)S(1)}, f32[10,2,8,128]{3,2,1,0:T(8,128)S(1)}, u32[]{:S(2)}, u32[]{:S(2)}) %collective-permute-start) | collective-permute-done | bytes 81952 | tf_op jit(solution)/shard_map/ppermute | solution.py:364
  9.8 0.6 copy-done.2
  10.4 1.7 %y_slab_kernel.1 = (f32[160,128]{1,0:T(8,128)}, f32[160,128]{1,0:T(8,128)}) custom-call(f32[10,4,8,128]{3,2,1,0:T(8,128)} %h.7, f32[10,2,8,128]{3,2,1,0:T(8,128)} %copy-done.2, f32[10,2,8,128]{3,2,1,0:T(8,128)} %copy-done.1), custom_call_target="tpu_custom_call" | custom-call | tf_op jit(solution)/shard_map/y_slab_kernel/pallas_call | solution.py:367
  12.2 4.6 %collective-permute-start.2 = (f32[160,128]{1,0:T(8,128)}, f32[160,128]{1,0:T(8,128)S(1)}, u32[]{:S(2)}, u32[]{:S(2)}) collective-permute-start(f32[160,128]{1,0:T(8,128)} %get-tuple-element.9), channel_id=1, source_target_pairs={{0,32},{32,64},{64,96},{1,33},{33,65},{65,97},{2,34},{34,66},{66,9... | collective-permute-start | bytes 245768 | tf_op jit(solution)/shard_map/ppermute | solution.py:369
  16.8 0.0 copy-start.5
  16.8 5.1 %collective-permute-start.3 = (f32[160,128]{1,0:T(8,128)}, f32[160,128]{1,0:T(8,128)S(1)}, u32[]{:S(2)}, u32[]{:S(2)}) collective-permute-start(f32[160,128]{1,0:T(8,128)} %get-tuple-element.10), channel_id=1, source_target_pairs={{32,0},{64,32},{96,64},{33,1},{65,33},{97,65},{34,2},{66,34},{98,6... | collective-permute-start | bytes 245768 | tf_op jit(solution)/shard_map/ppermute | solution.py:370
  21.9 0.0 collective-permute-done.2.yl
  21.9 1.1 %collective-permute-done.3.yh = f32[160,128]{1,0:T(8,128)S(1)} collective-permute-done((f32[160,128]{1,0:T(8,128)}, f32[160,128]{1,0:T(8,128)S(1)}, u32[]{:S(2)}, u32[]{:S(2)}) %collective-permute-start.3) | collective-permute-done | bytes 81952 | tf_op jit(solution)/shard_map/ppermute | solution.py:370
  23.0 0.6 copy-done.4
  23.6 2.1 %x_edge_kernel.1 = (f32[2,960]{1,0:T(2,128)}, f32[2,960]{1,0:T(2,128)}) custom-call(f32[10,4,8,128]{3,2,1,0:T(8,128)} %h.7, f32[10,2,8,128]{3,2,1,0:T(8,128)} %copy-done.2, f32[10,2,8,128]{3,2,1,0:T(8,128)} %copy-done.1, f32[160,128]{1,0:T(8,128)} %copy-done.3, f32[160,128]{1,0:T(8,128)} %copy-done.4), custom_call_target="tpu_custom_call" | custom-call | tf_op jit(solution)/shard_map/x_edge_kernel/pallas_call | solution.py:373
  25.8 2.9 %collective-permute-start.4 = (f32[2,960]{1,0:T(2,128)}, f32[2,960]{1,0:T(2,128)S(1)}, u32[]{:S(2)}, u32[]{:S(2)}) collective-permute-start(f32[2,960]{1,0:T(2,128)} %get-tuple-element.12), channel_id=1, source_target_pairs={{0,128},{128,256},{256,384},{1,129},{129,257},{257,385},{2,130},{1... | collective-permute-start | bytes 23048 | tf_op jit(solution)/shard_map/ppermute | solution.py:375
  28.6 1.3 %collective-permute-start.5 = (f32[2,960]{1,0:T(2,128)}, f32[2,960]{1,0:T(2,128)S(1)}, u32[]{:S(2)}, u32[]{:S(2)}) collective-permute-start(f32[2,960]{1,0:T(2,128)} %get-tuple-element.13), channel_id=1, source_target_pairs={{128,0},{256,128},{384,256},{129,1},{257,129},{385,257},{130,2},{2... | collective-permute-start | bytes 23048 | tf_op jit(solution)/shard_map/ppermute | solution.py:376
  29.9 0.7 reshape.17.coef
  30.6 2.3 %interior_points_kernel.1.inner = f32[10,128]{1,0:T(8,128)} custom-call(f32[10,4,8,128]{3,2,1,0:T(8,128)} %h.7, f32[10,2,8,128]{3,2,1,0:T(8,128)} %copy-done.2, f32[10,2,8,128]{3,2,1,0:T(8,128)} %copy-done.1, f32[160,128]{1,0:T(8,128)} %copy-done.3, f32[160,128]{1,0:T(8,128)} %copy-done.4, s32[3,128]{1,0:T(4,128)} %cells.3, f32[3,128]{1,0:T(4,128)} %frac.3), custom_call_target="tpu_custom_call" | custom-call | tf_op jit(solution)/shard_map/interior_points_kernel/pallas_call | solution.py:377
  32.9 0.0 collective-permute-done.4.xl
  32.9 0.4 collective-permute-done.5.xr
  33.2 0.2 copy-done.6
  33.5 0.4 copy-done.7
  33.8 2.2 %pack_kernel.1 = bf16[32,56,128]{2,1,0:T(8,128)(2,1)} custom-call(f32[10,128]{1,0:T(8,128)} %interior_points_kernel.1.inner, f32[2,960]{1,0:T(2,128)} %copy-done.6, f32[2,960]{1,0:T(2,128)} %copy-done.7, s32[3,128]{1,0:T(4,128)} %cells.3, f32[3,128]{1,0:T(4,128)} %frac.3, s32[1,128]{1,0:T(1,128)} %bitcast.12, f32[40,128]{1,0:T(8,128)} %reshape.17.coef), custom_call_target="tpu_custom_call" | custom-call | tf_op jit(solution)/shard_map/pack_kernel/pallas_call | solution.py:384
  36.1 37.0 %all_to_all.10.arrived = bf16[32,56,128]{2,1,0:T(8,128)(2,1)} all-to-all(bf16[32,56,128]{2,1,0:T(8,128)(2,1)} %pack_kernel.1), channel_id=1, replica_groups=mesh['gx'=4,'gy'=4,'gz'=32] {'gz'}, dimensions={0} | all-to-all | bytes 917504 | tf_op jit(solution)/shard_map/all_to_all | solution.py:395
  73.1 3.4 %partial_modes_kernel.1 = bf16[16,80,128]{2,1,0:T(8,128)(2,1)} custom-call(bf16[32,56,128]{2,1,0:T(8,128)(2,1)} %all_to_all.10.arrived, f32[32,1024]{1,0:T(8,128)} %constant.4.clone.radial, bf16[128,1024]{1,0:T(8,128)(2,1)} %constant.5.clone.angular), custom_call_target="tpu_custom_call" | custom-call | tf_op jit(solution)/shard_map/partial_modes_kernel/pallas_call | solution.py:397
  76.5 6.6 %all-to-all-start.1 = ((bf16[16,80,128]{2,1,0:T(8,128)(2,1)}), bf16[16,80,128]{2,1,0:T(8,128)(2,1)S(1)}, u32[]{:S(2)}, u32[]{:S(2)}) async-start(bf16[16,80,128]{2,1,0:T(8,128)(2,1)} %partial_modes_kernel.1), calls=%async_computation.1 | async-start | bytes 655360 | tf_op jit(solution)/shard_map/all_to_all | solution.py:403
  83.0 2.2 %right_side_kernel.1 = (f32[10,4,8,128]{3,2,1,0:T(8,128)}, f32[10,4,8,128]{3,2,1,0:T(8,128)}) custom-call(f32[10,4,8,128]{3,2,1,0:T(8,128)} %h.7, f32[10,2,8,128]{3,2,1,0:T(8,128)} %copy-done.2, f32[10,2,8,128]{3,2,1,0:T(8,128)} %copy-done.1, f32[160,128]{1,0:T(8,128)} %copy-done.3, f32[160,128]{1,0:T(8,128)} %copy-done.4, f32[10,4,8,128]{3,2,1,0:T(8,128)} %p.1, ...), custom_call_target="tpu_custom_call" | custom-call | tf_op jit(solution)/shard_map/right_side_kernel/pallas_call | solution.py:381
  85.2 2.5 %source_kernel.1 = f32[10,4,8,128]{3,2,1,0:T(8,128)} custom-call(s32[8]{0:T(128)} %bitcast.13, bf16[32,56,128]{2,1,0:T(8,128)(2,1)} %all_to_all.10.arrived, f32[3,8,128]{2,1,0:T(8,128)} %bitcast.10, s32[8,128]{1,0:T(8,128)} %bitcast.11, f32[10,4,8,128]{3,2,1,0:T(8,128)} %get-tuple-element.14.partial, f32[2,960]{1,0:T(2,128)} %copy-done.6, f32[2,960]{1,0:T(2,128)} %copy-done.7), custom_call_target="tpu_custom_call" | custom-call | tf_op jit(solution)/shard_map/source_kernel/pallas_call | solution.py:404
  87.8 2.9 %all-to-all-done.1.arrived = bf16[16,80,128]{2,1,0:T(8,128)(2,1)S(1)} async-done(((bf16[16,80,128]{2,1,0:T(8,128)(2,1)}), bf16[16,80,128]{2,1,0:T(8,128)(2,1)S(1)}, u32[]{:S(2)}, u32[]{:S(2)}) %all-to-all-start.1) | async-done | bytes 327712 | tf_op jit(solution)/shard_map/all_to_all | solution.py:403
  90.7 0.7 copy-done
  91.4 1.7 %sum_modes_kernel.1 = f32[10,1,961]{2,1,0:T(1,128)} custom-call(bf16[16,80,128]{2,1,0:T(8,128)(2,1)} %copy-done), custom_call_target="tpu_custom_call" | custom-call | tf_op jit(solution)/shard_map/sum_modes_kernel/pallas_call | solution.py:423
  (9 shorter events, 0.0 us)
Async XLA Ops:
  1.6 6.8 %collective-permute-start.1 = (f32[10,2,8,128]{3,2,1,0:T(8,128)S(1)}, f32[10,2,8,128]{3,2,1,0:T(8,128)S(1)}, u32[]{:S(2)}, u32[]{:S(2)}) collective-permute-start(f32[10,2,8,128]{3,2,1,0:T(8,128)S(1)} %get-tuple-element.15), channel_id=1, source_target_pairs={{1,0},{2,1},{3,2},{4,3},{5,4},{6,5},{7,6},{8,7},{9,8},{10,9},{11,1... | collective-permute-start | bytes 245768 | tf_op jit(solution)/shard_map/ppermute | solution.py:365
  2.9 6.9 %collective-permute-start = (f32[10,2,8,128]{3,2,1,0:T(8,128)S(1)}, f32[10,2,8,128]{3,2,1,0:T(8,128)S(1)}, u32[]{:S(2)}, u32[]{:S(2)}) collective-permute-start(f32[10,2,8,128]{3,2,1,0:T(8,128)S(1)} %get-tuple-element.16), channel_id=1, source_target_pairs={{0,1},{1,2},{2,3},{3,4},{4,5},{5,6},{6,7},{7,8},{8,9},{9,10},{10,1... | collective-permute-start | bytes 245768 | tf_op jit(solution)/shard_map/ppermute | solution.py:364
  8.3 1.5 %copy-start.1 = (f32[10,2,8,128]{3,2,1,0:T(8,128)}, f32[10,2,8,128]{3,2,1,0:T(8,128)S(1)}, u32[]{:S(2)}) copy-start(f32[10,2,8,128]{3,2,1,0:T(8,128)S(1)} %collective-permute-done.1.zh) | copy-start | bytes 245764
  9.8 0.6 copy-start.2
  12.2 9.7 %collective-permute-start.2 = (f32[160,128]{1,0:T(8,128)}, f32[160,128]{1,0:T(8,128)S(1)}, u32[]{:S(2)}, u32[]{:S(2)}) collective-permute-start(f32[160,128]{1,0:T(8,128)} %get-tuple-element.9), channel_id=1, source_target_pairs={{0,32},{32,64},{64,96},{1,33},{33,65},{65,97},{2,34},{34,66},{66,9... | collective-permute-start | bytes 245768 | tf_op jit(solution)/shard_map/ppermute | solution.py:369
  16.8 13.2 %copy-start.5 = (f32[1,10,8,64]{3,2,1,0:T(8,128)S(1)}, f32[1,10,8,64]{3,2,1,0:T(8,128)}, u32[]{:S(2)}) copy-start(f32[1,10,8,64]{3,2,1,0:T(8,128)} %param.20) | copy-start | bytes 61444
  16.8 6.2 %collective-permute-start.3 = (f32[160,128]{1,0:T(8,128)}, f32[160,128]{1,0:T(8,128)S(1)}, u32[]{:S(2)}, u32[]{:S(2)}) collective-permute-start(f32[160,128]{1,0:T(8,128)} %get-tuple-element.10), channel_id=1, source_target_pairs={{32,0},{64,32},{96,64},{33,1},{65,33},{97,65},{34,2},{66,34},{98,6... | collective-permute-start | bytes 245768 | tf_op jit(solution)/shard_map/ppermute | solution.py:370
  21.9 1.1 %copy-start.3 = (f32[160,128]{1,0:T(8,128)}, f32[160,128]{1,0:T(8,128)S(1)}, u32[]{:S(2)}) copy-start(f32[160,128]{1,0:T(8,128)S(1)} %collective-permute-done.2.yl) | copy-start | bytes 245764
  23.0 0.6 copy-start.4
  25.8 7.1 %collective-permute-start.4 = (f32[2,960]{1,0:T(2,128)}, f32[2,960]{1,0:T(2,128)S(1)}, u32[]{:S(2)}, u32[]{:S(2)}) collective-permute-start(f32[2,960]{1,0:T(2,128)} %get-tuple-element.12), channel_id=1, source_target_pairs={{0,128},{128,256},{256,384},{1,129},{129,257},{257,385},{2,130},{1... | collective-permute-start | bytes 23048 | tf_op jit(solution)/shard_map/ppermute | solution.py:375
  28.6 4.6 %collective-permute-start.5 = (f32[2,960]{1,0:T(2,128)}, f32[2,960]{1,0:T(2,128)S(1)}, u32[]{:S(2)}, u32[]{:S(2)}) collective-permute-start(f32[2,960]{1,0:T(2,128)} %get-tuple-element.13), channel_id=1, source_target_pairs={{128,0},{256,128},{384,256},{129,1},{257,129},{385,257},{130,2},{2... | collective-permute-start | bytes 23048 | tf_op jit(solution)/shard_map/ppermute | solution.py:376
  32.9 0.6 copy-start.6
  33.2 0.6 copy-start.7
  76.5 14.2 %all-to-all-start.1 = ((bf16[16,80,128]{2,1,0:T(8,128)(2,1)}), bf16[16,80,128]{2,1,0:T(8,128)(2,1)S(1)}, u32[]{:S(2)}, u32[]{:S(2)}) async-start(bf16[16,80,128]{2,1,0:T(8,128)(2,1)} %partial_modes_kernel.1), calls=%async_computation.1 | async-start | bytes 655360 | tf_op jit(solution)/shard_map/all_to_all | solution.py:403
  90.7 0.7 copy-start

commit v2 on v1

--- a/solution.py
+++ b/solution.py
@@ -26,9 +26,11 @@
 MODE_TILES = 8
 MODE_ROWS = COMP * MODE_TILES
 CHEB = 8
-COEF_ROWS = COMP * CHEB * CHEB * CHEB // LANES
-POINT_ROWS = 16
+HALF = COMP // 2
+POINT_ROWS = COMP + 2
+SENT_ROWS = 32
 SLOTS = 8
+VMEM_GRANT = 8 << 20
 
 F32 = jnp.float32
 BF16 = jnp.bfloat16
@@ -160,7 +162,7 @@
     out[...] = weighted_rows(parts, cell, fraction)
 
 
-def pack_kernel(inner, xl, xr, cells, frac, points, coef, out):
+def pack_kernel(core, inner, xl, xr, cells, frac, points, coef, out):
     cell, fraction = cells[...], frac[...]
     edges = jnp.concatenate([xl[...], xr[...]], axis=0)
     place = iota((4, LANES), 0)
@@ -174,13 +176,19 @@
     sphere = point // NANG
     polar = (point // NPHI % NTHETA).astype(F32)
     azimuth = (point % NPHI).astype(F32)
-    tail = jnp.zeros((POINT_ROWS - COMP - 2, LANES), F32)
-    coefficients = coef[...].astype(BF16)
+    quarter = [
+        jnp.concatenate(
+            [jnp.where(core[0] == 0, coef[c, 0:4, :], coef[c, 4:8, :]) for c in (a, a + HALF)],
+            axis=1,
+        )
+        for a in range(HALF)
+    ]
+    main = jnp.concatenate(quarter[:4], axis=0).astype(BF16)
     for s in range(out.shape[0]):
         node = jnp.where(sphere == s, polar, 255.0)
-        block = jnp.concatenate([values, node, azimuth, tail], axis=0)
-        out[s, 0:POINT_ROWS, :] = block.astype(BF16)
-        out[s, POINT_ROWS : POINT_ROWS + COEF_ROWS, :] = coefficients
+        block = jnp.concatenate([values, node, azimuth, quarter[4]], axis=0)
+        out[s, 0:16, :] = block.astype(BF16)
+        out[s, 16:32, :] = main
 
 
 def partial_modes_kernel(arrived, radial, angular, out, rows):
@@ -190,7 +198,7 @@
     for s in range(0, arrived.shape[0], 2):
         left, right = [], []
         for k in (s, s + 1):
-            block = arrived[k, 0:POINT_ROWS, :].astype(F32)
+            block = arrived[k, 0:16, :].astype(F32)
             at_i = row_i == block[COMP : COMP + 1]
             at_j = row_j == block[COMP + 1 : COMP + 2]
             left.append(
@@ -257,7 +265,9 @@
             out[c, z] = momentum + HALF_STEP * (laplacian - potential[z] * coupled)
 
 
-def source_kernel(patch, arrived, coords, cells, partial, xl, xr, out, series, terms, sources):
+def source_kernel(
+    core, patch, mine, other, coords, cells, partial, xl, xr, out, series, terms, sources
+):
     for axis in range(3):
         value = coords[axis]
         older, newer = jnp.ones_like(value), value
@@ -272,21 +282,28 @@
         )
         high, low = split2(product)
         empty = jnp.zeros((CHEB * CHEB, LANES), BF16)
-        block = arrived[patch[slot], POINT_ROWS : POINT_ROWS + COEF_ROWS, :]
-        grown = jnp.zeros((COEF_ROWS, 2 * LANES), F32)
+        chosen = patch[slot]
+        first, second = mine[chosen], other[chosen]
+        block = jnp.concatenate([first[16:32], second[16:32], first[0:16], second[0:16]], axis=0)
+        grown = jnp.zeros((64, 2 * LANES), F32)
         for part in (high, low):
             wide = jnp.concatenate(
                 [jnp.concatenate([part, empty], axis=0), jnp.concatenate([empty, part], axis=0)],
                 axis=1,
             )
             grown += dot(block, wide, NN)
-        even = series[0, pl.ds(slot, 4, stride=2 * SLOTS), :]
-        odd = series[0, pl.ds(slot + SLOTS, 4, stride=2 * SLOTS), :]
-        even = jnp.concatenate([even] * COMP, axis=0)
-        odd = jnp.concatenate([odd] * COMP, axis=0)
-        terms[slot * COEF_ROWS : (slot + 1) * COEF_ROWS, :] = (
-            grown[:, :LANES] * even + grown[:, LANES:] * odd
-        )
+        start = series[0, pl.ds(slot, 4, stride=SLOTS), :]
+        end = series[0, pl.ds(slot + 4 * SLOTS, 4, stride=SLOTS), :]
+        near = jnp.where(core[0] == 0, start, end)
+        far = jnp.where(core[0] == 0, end, start)
+        near, far = jnp.concatenate([near] * 4, axis=0), jnp.concatenate([far] * 4, axis=0)
+        for side in range(2):
+            lanes = slice(side * LANES, (side + 1) * LANES)
+            main = grown[0:16, lanes] * near + grown[16:32, lanes] * far
+            rest = grown[44:48, lanes] * near[0:4] + grown[60:64, lanes] * far[0:4]
+            row = (slot * 2 + side) * 20
+            terms[row : row + 16, :] = main
+            terms[row + 16 : row + 20, :] = rest
     count = SLOTS * COMP
     total = terms[pl.ds(0, count, stride=4), :]
     for m in range(1, 4):
@@ -332,6 +349,7 @@
         in_specs=specs,
         scratch_shapes=scratch,
         name=kernel.__name__,
+        compiler_params=pltpu.CompilerParams(vmem_limit_bytes=VMEM_GRANT),
     )
 
 
@@ -359,6 +377,7 @@
     sph_frac,
 ):
     z_count = lax.axis_size("gz")
+    core = (lax.axis_index("gy") % 2).reshape(1)
     xy_count = lax.axis_size("gx") * lax.axis_size("gy")
     up, down = neighbours("gz")
     zl = lax.ppermute(field_h[:, CZ - 2 :], "gz", up)
@@ -382,17 +401,19 @@
         *grid, field_p, potential, coupling
     )
     packed = call(
-        pack_kernel, shape((z_count, POINT_ROWS + COEF_ROWS, LANES), BF16), count=7
+        pack_kernel, shape((z_count, SENT_ROWS, LANES), BF16), count=8, smem=(0,)
     )(
+        core,
         inner,
         xl,
         xr,
         sph_cells,
         sph_frac,
         sph_points.reshape(1, LANES),
-        patch_coef.reshape(COEF_ROWS, LANES),
+        patch_coef[0],
     )
     arrived = lax.all_to_all(packed, "gz", 0, 0, tiled=True)
+    partner = lax.ppermute(arrived, "gy", [(i, i ^ 1) for i in range(lax.axis_size("gy"))])
     radial, angular = mode_factors()
     sent = call(
         partial_modes_kernel,
@@ -406,14 +427,16 @@
         cube,
         scratch=[
             pltpu.VMEM((3, CHEB * SLOTS, LANES), F32),
-            pltpu.VMEM((SLOTS * COEF_ROWS, LANES), F32),
+            pltpu.VMEM((SLOTS * 40, LANES), F32),
             pltpu.VMEM((SLOTS * COMP, LANES), F32),
         ],
-        count=7,
-        smem=(0,),
+        count=9,
+        smem=(0, 1),
     )(
+        core,
         wt_patch.reshape(SLOTS),
         arrived,
+        partner,
         jnp.moveaxis(wt_coords[0, 0, 0], 1, 0),
         wt_cells[0, 0, 0],
         partial,

time: 93.8 us -> 80.9 us (0.86)
  Pallas kernels: 18.1 us -> 8.16 us
  blocking collectives: 37 us -> 33.9 us
  starting transfers between devices: 27.1 us -> 28.9 us
  local copies, waits for them, and re-layouts: 4.23 us -> 3.03 us
    all_to_all x1, blocking collectives: 37 us -> 33.9 us  [shards(): arrived = lax.all_to_all(packed, 'gz', 0, 0, tiled=True)]
    ppermute x0 -> x1, starting transfers between devices: none -> 2.01 us  [shards(): lax.ppermute(arrived, 'gy', [(i, i ^ 1) for i in range(lax.axis_size('gy'...]
    pallas_call x1, Pallas kernels: 2.12 us -> 0.4 us  [shards(): first, last = call(x_edge_kernel, (edge, edge), count=5)(*grid)]
    pallas_call x1, Pallas kernels: 2.26 us -> 0.55 us  [shards(): call(interior_points_kernel, shape((COMP, LANES)), count=7)]
    pallas_call x1, Pallas kernels: 1.72 us -> 0.06 us  [shards(): first, last = call(y_slab_kernel, (slab, slab), count=3)(field_h, zl, zh)]
    all_to_all x1, waiting for transfers between devices: 2.93 us -> 1.33 us  [shards(): gathered = lax.all_to_all(sent, ('gx', 'gy'), 0, 0, tiled=True)]
    pallas_call x1, Pallas kernels: 2.24 us -> 0.64 us  [shards(): call(pack_kernel, shape((z_count, SENT_ROWS, LANES), BF16), count=8, smem...]
    ppermute x1, waiting for transfers between devices: 0.35 us -> 1.81 us  [shards(): xr = lax.ppermute(first, 'gx', down)]
  transfers between devices with their start and end apart: 7 -> 8, of which waited for: 4 -> 4; matrix products, arithmetic and copies ran while one was open for 1% -> 0% of each run, Pallas kernels for 8% -> 5%
where the time goes in v2:
time: 80.9 us; the launch traced here: 80.4 us
  blocking collectives  33.9 us (42%)
  starting transfers between devices  28.9 us (36%)
  Pallas kernels  8.16 us (10%)
  waiting for transfers between devices  5.6 us (7%)
  local copies, waits for them, and re-layouts  3.03 us (4%)
  between operations  0.83 us (1%)
    all_to_all x1, blocking collectives, shards(): arrived = lax.all_to_all(packed, 'gz', 0, 0, tiled=True)  33.9 us
    all_to_all x1, starting transfers between devices, shards(): gathered = lax.all_to_all(sent, ('gx', 'gy'), 0, 0, tiled=True)  5.96 us
    ppermute x1, starting transfers between devices, shards(): zl = lax.ppermute(field_h[:, CZ - 2:], 'gz', up)  5.45 us
    ppermute x1, starting transfers between devices, shards(): yh = lax.ppermute(first, 'gy', down)  5.1 us
    ppermute x1, starting transfers between devices, shards(): yl = lax.ppermute(last, 'gy', up)  4.62 us
    ppermute x1, starting transfers between devices, shards(): xl = lax.ppermute(last, 'gx', up)  3.13 us
    pallas_call x1, Pallas kernels, shards(): call(partial_modes_kernel, shape((xy_count, MODE_ROWS, LANES), BF16), scr...  2.22 us
    unnamed x26, local copies, waits for them, and re-layouts  2.05 us
  transfers between devices with their start and end apart: 8, of which 4 were waited for; matrix products, arithmetic and copies ran while one was open for 0% of the time, Pallas kernels for 5%

profile of v2, /device:TPU:1, one launch (start us, length us, event | category | flops | bytes accessed | tf_op | source)
XLA Modules:
  0.0 80.4 jit_solution(13696409898893610679)
XLA Ops:
  0.6 1.0 %fusion = (f32[10,2,8,128]{3,2,1,0:T(8,128)S(1)}, f32[10,2,8,128]{3,2,1,0:T(8,128)S(1)}) fusion(f32[10,4,8,128]{3,2,1,0:T(8,128)} %h.7), kind=kLoop, calls=%fused_computation | loop fusion | bytes 327680 | tf_op jit(solution)/shard_map/slice | solution.py:384
  1.6 1.3 %collective-permute-start.1 = (f32[10,2,8,128]{3,2,1,0:T(8,128)S(1)}, f32[10,2,8,128]{3,2,1,0:T(8,128)S(1)}, u32[]{:S(2)}, u32[]{:S(2)}) collective-permute-start(f32[10,2,8,128]{3,2,1,0:T(8,128)S(1)} %get-tuple-element.15), channel_id=1, source_target_pairs={{1,0},{2,1},{3,2},{4,3},{5,4},{6,5},{7,6},{8,7},{9,8},{10,9},{11,1... | collective-permute-start | bytes 245768 | tf_op jit(solution)/shard_map/ppermute | solution.py:384
  2.9 5.4 %collective-permute-start = (f32[10,2,8,128]{3,2,1,0:T(8,128)S(1)}, f32[10,2,8,128]{3,2,1,0:T(8,128)S(1)}, u32[]{:S(2)}, u32[]{:S(2)}) collective-permute-start(f32[10,2,8,128]{3,2,1,0:T(8,128)S(1)} %get-tuple-element.16), channel_id=1, source_target_pairs={{0,1},{1,2},{2,3},{3,4},{4,5},{5,6},{6,7},{7,8},{8,9},{9,10},{10,1... | collective-permute-start | bytes 245768 | tf_op jit(solution)/shard_map/ppermute | solution.py:383
  8.4 0.0 collective-permute-done.1.zh
  8.4 1.5 %collective-permute-done.zl = f32[10,2,8,128]{3,2,1,0:T(8,128)S(1)} collective-permute-done((f32[10,2,8,128]{3,2,1,0:T(8,128)S(1)}, f32[10,2,8,128]{3,2,1,0:T(8,128)S(1)}, u32[]{:S(2)}, u32[]{:S(2)}) %collective-permute-start) | collective-permute-done | bytes 81952 | tf_op jit(solution)/shard_map/ppermute | solution.py:383
  9.8 0.1 y_slab_kernel.1
  9.9 4.6 %collective-permute-start.2 = (f32[160,128]{1,0:T(8,128)S(1)}, f32[160,128]{1,0:T(8,128)S(1)}, u32[]{:S(2)}, u32[]{:S(2)}) collective-permute-start(f32[160,128]{1,0:T(8,128)S(1)} %get-tuple-element.9), channel_id=1, source_target_pairs={{0,32},{32,64},{64,96},{1,33},{33,65},{65,97},{2,34},{34,66},{66,9... | collective-permute-start | bytes 245768 | tf_op jit(solution)/shard_map/ppermute | solution.py:388
  14.5 5.1 %collective-permute-start.3 = (f32[160,128]{1,0:T(8,128)S(1)}, f32[160,128]{1,0:T(8,128)S(1)}, u32[]{:S(2)}, u32[]{:S(2)}) collective-permute-start(f32[160,128]{1,0:T(8,128)S(1)} %get-tuple-element.10), channel_id=1, source_target_pairs={{32,0},{64,32},{96,64},{33,1},{65,33},{97,65},{34,2},{66,34},{98,6... | collective-permute-start | bytes 245768 | tf_op jit(solution)/shard_map/ppermute | solution.py:389
  19.7 1.0 %collective-permute-done.3.yh = f32[160,128]{1,0:T(8,128)S(1)} collective-permute-done((f32[160,128]{1,0:T(8,128)S(1)}, f32[160,128]{1,0:T(8,128)S(1)}, u32[]{:S(2)}, u32[]{:S(2)}) %collective-permute-start.3) | collective-permute-done | bytes 81952 | tf_op jit(solution)/shard_map/ppermute | solution.py:389
  20.6 0.4 x_edge_kernel.1
  21.1 3.1 %collective-permute-start.4 = (f32[2,960]{1,0:T(2,128)S(1)}, f32[2,960]{1,0:T(2,128)S(1)}, u32[]{:S(2)}, u32[]{:S(2)}) collective-permute-start(f32[2,960]{1,0:T(2,128)S(1)} %get-tuple-element.12), channel_id=1, source_target_pairs={{0,128},{128,256},{256,384},{1,129},{129,257},{257,385},{2,130},{1... | collective-permute-start | bytes 23048 | tf_op jit(solution)/shard_map/ppermute | solution.py:394
  24.2 1.3 %collective-permute-start.5 = (f32[2,960]{1,0:T(2,128)S(1)}, f32[2,960]{1,0:T(2,128)S(1)}, u32[]{:S(2)}, u32[]{:S(2)}) collective-permute-start(f32[2,960]{1,0:T(2,128)S(1)} %get-tuple-element.13), channel_id=1, source_target_pairs={{128,0},{256,128},{384,256},{129,1},{257,129},{385,257},{130,2},{2... | collective-permute-start | bytes 23048 | tf_op jit(solution)/shard_map/ppermute | solution.py:395
  25.5 0.0 copy-start.9
  25.5 0.0 copy-start.8
  25.5 0.7 copy-done.9
  26.2 0.0 copy-done.8
  26.2 0.6 interior_points_kernel.1.inner
  26.8 1.8 %collective-permute-done.5.xr = f32[2,960]{1,0:T(2,128)S(1)} collective-permute-done((f32[2,960]{1,0:T(2,128)S(1)}, f32[2,960]{1,0:T(2,128)S(1)}, u32[]{:S(2)}, u32[]{:S(2)}) %collective-permute-start.5) | collective-permute-done | bytes 7712 | tf_op jit(solution)/shard_map/ppermute | solution.py:395
  28.6 0.7 copy-done.11
  29.2 0.6 pack_kernel.1
  29.9 0.0 copy-start.1
  29.9 0.0 copy-start.3
  29.9 33.9 %all_to_all.10.mine.arrived = bf16[32,32,128]{2,1,0:T(8,128)(2,1)S(1)} all-to-all(bf16[32,32,128]{2,1,0:T(8,128)(2,1)S(1)} %pack_kernel.1), channel_id=1, replica_groups=mesh['gx'=4,'gy'=4,'gz'=32] {'gz'}, dimensions={0} | all-to-all | bytes 524288 | tf_op jit(solution)/shard_map/all_to_all | solution.py:415
  63.9 2.2 %partial_modes_kernel.1 = bf16[16,80,128]{2,1,0:T(8,128)(2,1)} custom-call(bf16[32,32,128]{2,1,0:T(8,128)(2,1)S(1)} %all_to_all.10.mine.arrived, f32[32,1024]{1,0:T(8,128)S(1)} %copy-done.3, bf16[128,1024]{1,0:T(8,128)(2,1)S(1)} %copy-done.1), custom_call_target="tpu_custom_call" | custom-call | tf_op jit(solution)/shard_map/partial_modes_kernel/pallas_call | solution.py:418
  66.1 6.0 %all-to-all-start.1 = ((bf16[16,80,128]{2,1,0:T(8,128)(2,1)}), bf16[16,80,128]{2,1,0:T(8,128)(2,1)S(1)}, u32[]{:S(2)}, u32[]{:S(2)}) async-start(bf16[16,80,128]{2,1,0:T(8,128)(2,1)} %partial_modes_kernel.1), calls=%async_computation.1 | async-start | bytes 655360 | tf_op jit(solution)/shard_map/all_to_all | solution.py:424
  72.1 2.0 %collective-permute-start.6 = (bf16[32,32,128]{2,1,0:T(8,128)(2,1)S(1)}, bf16[32,32,128]{2,1,0:T(8,128)(2,1)S(1)}, u32[]{:S(2)}, u32[]{:S(2)}) collective-permute-start(bf16[32,32,128]{2,1,0:T(8,128)(2,1)S(1)} %all_to_all.10.mine.arrived), channel_id=1, source_target_pairs={{0,32},{32,0},{64,96},{96,64},{1,33},{33,1},{65,97},{97,65},{2,34}... | collective-permute-start | bytes 786440 | tf_op jit(solution)/shard_map/ppermute | solution.py:416
  74.1 0.0 copy-start.6
  74.1 1.7 %right_side_kernel.1 = (f32[10,4,8,128]{3,2,1,0:T(8,128)}, f32[10,4,8,128]{3,2,1,0:T(8,128)S(1)}) custom-call(f32[10,4,8,128]{3,2,1,0:T(8,128)S(1)} %copy-done, f32[10,2,8,128]{3,2,1,0:T(8,128)S(1)} %collective-permute-done.zl, f32[10,2,8,128]{3,2,1,0:T(8,128)S(1)} %collective-permute-done.1.zh, f32[160,128]{1,0:T(8,128)S(1)} %collective-permute-done.2.yl, ...), custom_call_target="tpu_custom_call" | custom-call | tf_op jit(solution)/shard_map/right_side_kernel/pallas_call | solution.py:400
  75.8 0.7 copy-done.10
  76.5 1.9 %source_kernel.1 = f32[10,4,8,128]{3,2,1,0:T(8,128)} custom-call(s32[1]{0:T(128)} %bitcast.core, s32[8]{0:T(128)S(1)} %bitcast.13, bf16[32,32,128]{2,1,0:T(8,128)(2,1)S(1)} %all_to_all.10.mine.arrived, bf16[32,32,128]{2,1,0:T(8,128)(2,1)S(1)} %collective-permute-done.6.other, f32[3,8,128]{2,1,0:T(8,128)S(1)} %bitcast.10, s32[8,128]{1,0:T(8,128)S(1)} %bitcast.11, ...), custom_call_target="tpu_custom_call" | custom-call | tf_op jit(solution)/shard_map/source_kernel/pallas_call | solution.py:425
  78.4 1.3 %all-to-all-done.1.arrived = bf16[16,80,128]{2,1,0:T(8,128)(2,1)S(1)} async-done(((bf16[16,80,128]{2,1,0:T(8,128)(2,1)}), bf16[16,80,128]{2,1,0:T(8,128)(2,1)S(1)}, u32[]{:S(2)}, u32[]{:S(2)}) %all-to-all-start.1) | async-done | bytes 327712 | tf_op jit(solution)/shard_map/all_to_all | solution.py:424
  79.7 0.7 sum_modes_kernel.1
  (20 shorter events, 0.0 us)
Async XLA Ops:
  0.6 9.2 %copy-start = (f32[10,4,8,128]{3,2,1,0:T(8,128)S(1)}, f32[10,4,8,128]{3,2,1,0:T(8,128)}, u32[]{:S(2)}) copy-start(f32[10,4,8,128]{3,2,1,0:T(8,128)} %h.7) | copy-start | bytes 491524
  1.6 6.8 %collective-permute-start.1 = (f32[10,2,8,128]{3,2,1,0:T(8,128)S(1)}, f32[10,2,8,128]{3,2,1,0:T(8,128)S(1)}, u32[]{:S(2)}, u32[]{:S(2)}) collective-permute-start(f32[10,2,8,128]{3,2,1,0:T(8,128)S(1)} %get-tuple-element.15), channel_id=1, source_target_pairs={{1,0},{2,1},{3,2},{4,3},{5,4},{6,5},{7,6},{8,7},{9,8},{10,9},{11,1... | collective-permute-start | bytes 245768 | tf_op jit(solution)/shard_map/ppermute | solution.py:384
  2.9 6.9 %collective-permute-start = (f32[10,2,8,128]{3,2,1,0:T(8,128)S(1)}, f32[10,2,8,128]{3,2,1,0:T(8,128)S(1)}, u32[]{:S(2)}, u32[]{:S(2)}) collective-permute-start(f32[10,2,8,128]{3,2,1,0:T(8,128)S(1)} %get-tuple-element.16), channel_id=1, source_target_pairs={{0,1},{1,2},{2,3},{3,4},{4,5},{5,6},{6,7},{7,8},{8,9},{9,10},{10,1... | collective-permute-start | bytes 245768 | tf_op jit(solution)/shard_map/ppermute | solution.py:383
  9.9 9.7 %collective-permute-start.2 = (f32[160,128]{1,0:T(8,128)S(1)}, f32[160,128]{1,0:T(8,128)S(1)}, u32[]{:S(2)}, u32[]{:S(2)}) collective-permute-start(f32[160,128]{1,0:T(8,128)S(1)} %get-tuple-element.9), channel_id=1, source_target_pairs={{0,32},{32,64},{64,96},{1,33},{33,65},{65,97},{2,34},{34,66},{66,9... | collective-permute-start | bytes 245768 | tf_op jit(solution)/shard_map/ppermute | solution.py:388
  14.5 6.1 %collective-permute-start.3 = (f32[160,128]{1,0:T(8,128)S(1)}, f32[160,128]{1,0:T(8,128)S(1)}, u32[]{:S(2)}, u32[]{:S(2)}) collective-permute-start(f32[160,128]{1,0:T(8,128)S(1)} %get-tuple-element.10), channel_id=1, source_target_pairs={{32,0},{64,32},{96,64},{33,1},{65,33},{97,65},{34,2},{66,34},{98,6... | collective-permute-start | bytes 245768 | tf_op jit(solution)/shard_map/ppermute | solution.py:389
  21.1 5.7 %collective-permute-start.4 = (f32[2,960]{1,0:T(2,128)S(1)}, f32[2,960]{1,0:T(2,128)S(1)}, u32[]{:S(2)}, u32[]{:S(2)}) collective-permute-start(f32[2,960]{1,0:T(2,128)S(1)} %get-tuple-element.12), channel_id=1, source_target_pairs={{0,128},{128,256},{256,384},{1,129},{129,257},{257,385},{2,130},{1... | collective-permute-start | bytes 23048 | tf_op jit(solution)/shard_map/ppermute | solution.py:394
  24.2 4.4 %collective-permute-start.5 = (f32[2,960]{1,0:T(2,128)S(1)}, f32[2,960]{1,0:T(2,128)S(1)}, u32[]{:S(2)}, u32[]{:S(2)}) collective-permute-start(f32[2,960]{1,0:T(2,128)S(1)} %get-tuple-element.13), channel_id=1, source_target_pairs={{128,0},{256,128},{384,256},{129,1},{257,129},{385,257},{130,2},{2... | collective-permute-start | bytes 23048 | tf_op jit(solution)/shard_map/ppermute | solution.py:395
  25.5 0.7 copy-start.9
  25.5 0.7 copy-start.8
  26.2 2.4 %copy-start.4 = (f32[1,10,8,64]{3,2,1,0:T(8,128)S(1)}, f32[1,10,8,64]{3,2,1,0:T(8,128)}, u32[]{:S(2)}) copy-start(f32[1,10,8,64]{3,2,1,0:T(8,128)} %param.20) | copy-start | bytes 61444
  28.6 0.7 copy-start.11
  29.9 34.0 %copy-start.1 = (bf16[128,1024]{1,0:T(8,128)(2,1)S(1)}, bf16[128,1024]{1,0:T(8,128)(2,1)}, u32[]{:S(2)}) copy-start(bf16[128,1024]{1,0:T(8,128)(2,1)} %constant.24.clone.angular) | copy-start | bytes 786436
  29.9 34.0 %copy-start.3 = (f32[32,1024]{1,0:T(8,128)S(1)}, f32[32,1024]{1,0:T(8,128)}, u32[]{:S(2)}) copy-start(f32[32,1024]{1,0:T(8,128)} %constant.23.clone.radial) | copy-start | bytes 393220
  66.1 8.0 %copy-start.2 = (f32[10,4,8,128]{3,2,1,0:T(8,128)S(1)}, f32[10,4,8,128]{3,2,1,0:T(8,128)}, u32[]{:S(2)}) copy-start(f32[10,4,8,128]{3,2,1,0:T(8,128)} %p.1) | copy-start | bytes 491524
  66.1 8.0 %copy-start.5 = (f32[4,8,128]{2,1,0:T(8,128)S(1)}, f32[4,8,128]{2,1,0:T(8,128)}, u32[]{:S(2)}) copy-start(f32[4,8,128]{2,1,0:T(8,128)} %potential.1) | copy-start | bytes 49156
  66.1 8.0 %copy-start.7 = (f32[10,10]{1,0:T(8,128)S(1)}, f32[10,10]{1,0:T(8,128)}, u32[]{:S(2)}) copy-start(f32[10,10]{1,0:T(8,128)} %coupling.1) | copy-start | bytes 1204
  66.1 13.6 %all-to-all-start.1 = ((bf16[16,80,128]{2,1,0:T(8,128)(2,1)}), bf16[16,80,128]{2,1,0:T(8,128)(2,1)S(1)}, u32[]{:S(2)}, u32[]{:S(2)}) async-start(bf16[16,80,128]{2,1,0:T(8,128)(2,1)} %partial_modes_kernel.1), calls=%async_computation.1 | async-start | bytes 655360 | tf_op jit(solution)/shard_map/all_to_all | solution.py:424
  72.1 3.7 %collective-permute-start.6 = (bf16[32,32,128]{2,1,0:T(8,128)(2,1)S(1)}, bf16[32,32,128]{2,1,0:T(8,128)(2,1)S(1)}, u32[]{:S(2)}, u32[]{:S(2)}) collective-permute-start(bf16[32,32,128]{2,1,0:T(8,128)(2,1)S(1)} %all_to_all.10.mine.arrived), channel_id=1, source_target_pairs={{0,32},{32,0},{64,96},{96,64},{1,33},{33,1},{65,97},{97,65},{2,34}... | collective-permute-start | bytes 786440 | tf_op jit(solution)/shard_map/ppermute | solution.py:416
  74.1 1.7 %copy-start.6 = (f32[1,1,1,8,3,128]{5,3,4,2,1,0:T(8,128)S(1)}, f32[1,1,1,8,3,128]{5,3,4,2,1,0:T(8,128)}, u32[]{:S(2)}) copy-start(f32[1,1,1,8,3,128]{5,3,4,2,1,0:T(8,128)} %param.18) | copy-start | bytes 36868
  75.8 0.7 copy-start.10
  75.8 0.7 copy-start.12

commit v3 on v2

v3 whole, which is shorter than its diff:
```python
import functools

import jax
import jax.numpy as jnp
import numpy as np
from jax import lax
from jax.experimental import pallas as pl
from jax.experimental.pallas import tpu as pltpu
from jax.sharding import PartitionSpec as P

LMAX = 30
NTHETA = 32
NPHI = 64
NANG = NTHETA * NPHI
NMODE = (LMAX + 1) ** 2
HALF_STEP = 0.125

COMP = 10
CZ = 4
CY = 8
CX = 128
LANES = 128
ROWS_OWN = COMP * CZ * CY
ROWS_SLAB = COMP * 2 * CY
ROWS_ALL = ROWS_OWN + 4 * ROWS_SLAB
MODE_TILES = 8
MODE_ROWS = COMP * MODE_TILES
CHEB = 8
HALF = COMP // 2
POINT_ROWS = COMP + 2
SENT_ROWS = 32
SLOTS = 8
VMEM_GRANT = 8 << 20

F32 = jnp.float32
BF16 = jnp.bfloat16
HIGHEST = lax.Precision.HIGHEST
NN = (((1,), (0,)), ((), ()))
NT = (((1,), (1,)), ((), ()))
TN = (((0,), (0,)), ((), ()))


def mode_factors():
    polar = np.pi * (np.arange(NTHETA) + 0.5) / NTHETA
    azimuth = 2.0 * np.pi * np.arange(NPHI) / NPHI
    cosine, sine = np.cos(polar), np.sin(polar)
    legendre = np.zeros((LMAX + 1, LMAX + 1, NTHETA))
    diagonal = np.full(NTHETA, np.sqrt(0.25 / np.pi))
    for m in range(LMAX + 1):
        if m > 0:
            diagonal = diagonal * sine * np.sqrt((2.0 * m + 1.0) / (2.0 * m))
        legendre[m, m] = diagonal
        if m < LMAX:
            legendre[m + 1, m] = cosine * np.sqrt(2.0 * m + 3.0) * diagonal
        for l in range(m + 2, LMAX + 1):
            a = np.sqrt((4.0 * l * l - 1.0) / (l * l - m * m))
            b = np.sqrt(((l - 1.0) ** 2 - m * m) / (4.0 * (l - 1.0) ** 2 - 1.0))
            legendre[l, m] = a * (cosine * legendre[l - 1, m] - b * legendre[l - 2, m])
    width = MODE_TILES * LANES
    radial = np.zeros((NTHETA, width))
    angular = np.zeros((NPHI, width))
    weight = sine * np.pi / NTHETA
    for l in range(LMAX + 1):
        for m in range(-l, l + 1):
            n = l * l + l + m
            radial[:, n] = legendre[l, abs(m)] * weight
            if m == 0:
                angular[:, n] = 1.0
            elif m > 0:
                angular[:, n] = np.sqrt(2.0) * np.cos(m * azimuth)
            else:
                angular[:, n] = np.sqrt(2.0) * np.sin(-m * azimuth)
    angular = angular.astype(np.float32)
    high = angular.astype(jnp.bfloat16)
    low = (angular - high.astype(np.float32)).astype(jnp.bfloat16)
    return radial.astype(np.float32), np.concatenate([high, low], axis=0)


def iota(shape, dim):
    return lax.broadcasted_iota(jnp.int32, shape, dim)


def split2(value):
    high = value.astype(BF16)
    return high, (value - high.astype(F32)).astype(BF16)


def dot(a, b, dims, precision=None):
    return lax.dot_general(a, b, dims, precision=precision, preferred_element_type=F32)


def two_hot(position, cell, fraction):
    return jnp.where(position == cell, 1.0 - fraction, 0.0) + jnp.where(
        position == cell + 1, fraction, 0.0
    )


def weighted_rows(parts, plan):
    own, zl, zh, yl, yh = parts
    rows = []
    for c in range(COMP):
        total = jnp.zeros((8, LANES), F32)
        for z in range(CZ):
            base = (c * CZ + z) * CY
            total += own[base : base + 8] * plan[(z + 2) * 8 : (z + 3) * 8]
        for z in range(2):
            base = (c * 2 + z) * CY
            total += zl[base : base + 8] * plan[z * 8 : z * 8 + 8]
            total += zh[base : base + 8] * plan[(z + 6) * 8 : (z + 7) * 8]
            base = c * 16 + z * 8
            total += yl[base : base + 8] * plan[64 + z * 8 : 72 + z * 8]
            total += yh[base : base + 8] * plan[80 + z * 8 : 88 + z * 8]
        rows.append(jnp.sum(total, axis=0, keepdims=True))
    return jnp.concatenate(rows, axis=0)


def prep_kernel(
    core, cells, frac, points, coef, coords, wt_cells, p, v, k, q,
    wide, plan, node, main, rest, high, low, series, target,
):
    cell, fraction = cells[...], frac[...]
    wide_high, wide_low = split2(two_hot(iota((CX, LANES), 0) + 2, cell[2:3], fraction[2:3]))
    wide[0] = wide_high
    wide[1] = wide_low
    row8 = iota((8, LANES), 0)
    row16 = iota((16, LANES), 0)
    wy = two_hot(row8 + 2, cell[1:2], fraction[1:2])
    for z in range(CZ + 4):
        plan[z * 8 : z * 8 + 8, :] = two_hot(z, cell[0:1], fraction[0:1]) * wy
    wz = two_hot(row16 // 2, cell[0:1], fraction[0:1])
    plan[64:80, :] = wz * two_hot(row16 % 2, cell[1:2], fraction[1:2])
    plan[80:96, :] = wz * two_hot(row16 % 2 + CY + 2, cell[1:2], fraction[1:2])
    place = jnp.where(row8 < 2, row8, row8 + CX)
    plan[96:104, :] = two_hot(place, cell[2:3], fraction[2:3])
    point = points[...]
    node[0:1, :] = (point // NANG).astype(F32)
    node[1:2, :] = (point // NPHI % NTHETA).astype(F32)
    node[2:3, :] = (point % NPHI).astype(F32)
    quarter = [
        jnp.concatenate(
            [jnp.where(core[0] % 2 == 0, coef[c, 0:4, :], coef[c, 4:8, :]) for c in (a, a + HALF)],
            axis=1,
        )
        for a in range(HALF)
    ]
    main[...] = jnp.concatenate(quarter[:4], axis=0).astype(BF16)
    rest[...] = quarter[4]
    for axis in range(3):
        value = coords[axis]
        older, newer = jnp.ones_like(value), value
        for n in range(CHEB):
            series[axis, n * SLOTS : (n + 1) * SLOTS, :] = older
            older, newer = newer, 2.0 * value * newer - older
    for slot in range(SLOTS):
        third = series[2, pl.ds(slot, CHEB, stride=SLOTS), :]
        product = jnp.concatenate(
            [series[1, n * SLOTS + slot : n * SLOTS + slot + 1, :] * third for n in range(CHEB)],
            axis=0,
        )
        high[slot], low[slot] = split2(product)
    cell = wt_cells[...]
    target[0] = (cell // CX).astype(F32)
    target[1] = (cell % CX).astype(F32)


def edges_kernel(height, spot, h, zl, zh, base, plan, first, last, far, lower, upper):
    low, high = zl[...].astype(F32), zh[...].astype(F32)
    for c in range(COMP):
        for z in range(CZ + 4):
            if z < 2:
                source = low[(c * 2 + z) * CY : (c * 2 + z + 1) * CY]
            elif z < CZ + 2:
                source = h[c, z - 2]
            else:
                source = high[(c * 2 + z - 6) * CY : (c * 2 + z - 5) * CY]
            row = (c * (CZ + 4) + z) * 2
            lower[row : row + 2, :] = source[0:2]
            upper[row : row + 2, :] = source[CY - 2 : CY]
    below, above = lower[...].astype(BF16), upper[...].astype(BF16)
    first[...] = below
    last[...] = above
    row = iota((8, LANES), 0)
    lane = iota((8, LANES), 1)
    place = jnp.where(row < 2, row, row + CX - 4)
    pick = jnp.where(lane == place, 1.0, 0.0).astype(BF16)
    own = h[...].reshape(ROWS_OWN, LANES).astype(BF16)
    wide = jnp.concatenate([dot(pick, part, NT) for part in (own, zl[...], zh[...])], axis=1)
    empty = jnp.zeros((8, 2 * LANES - ROWS_SLAB), F32)

    def block(edge, start):
        tiles = edge.shape[1] // LANES
        rows = [
            edge[j : j + 1, t * LANES : (t + 1) * LANES]
            for j in (start, start + 1)
            for t in range(tiles)
        ]
        rows.append(jnp.zeros((16 - len(rows), LANES), F32))
        return jnp.concatenate(rows, axis=0).astype(BF16)

    below = jnp.concatenate([dot(pick, below, NT), empty], axis=1)
    above = jnp.concatenate([dot(pick, above, NT), empty], axis=1)
    blocks = [[block(edge, start) for start in (0, 2)] for edge in (wide, below, above)]
    column, level = spot[0] // height, spot[0] % height
    for e in range(far.shape[0]):
        right = e // height == column + 1
        inner, lower_row, upper_row = [jnp.where(right, hi, lo) for lo, hi in blocks]
        outer = jnp.where(e % height == level + 1, upper_row, lower_row)
        far[e] = jnp.where(e % height == level, inner, outer)


def middle_kernel(h, zl, zh, yl, yh, wide, plan, base, out, partial):
    high, low = split2(h[...].reshape(ROWS_OWN, LANES))
    near, fine = wide[0], wide[1]
    parts = [dot(high, near, NN) + dot(low, near, NN) + dot(high, fine, NN)]
    parts += [dot(slab[...], near, NN) + dot(slab[...], fine, NN) for slab in (zl, zh, yl, yh)]
    out[...] = weighted_rows(parts, plan[...])
    z_low, z_high = zl[...].astype(F32), zh[...].astype(F32)
    y_low, y_high = yl[...].astype(F32), yh[...].astype(F32)
    gap = jnp.zeros((CY - 4, LANES), F32)
    for c in range(COMP):
        at = c * 2 * CY
        two_back, one_back = z_low[at : at + CY], z_low[at + CY : at + 2 * CY]
        one_on, two_on = z_high[at : at + CY], z_high[at + CY : at + 2 * CY]
        along_z = [16.0 * one_back - two_back, -one_back, -one_on, 16.0 * one_on - two_on]
        for z in range(CZ):
            at = (c * (CZ + 4) + z + 2) * 2
            below, above = y_low[at : at + 2], y_high[at : at + 2]
            along_y = jnp.concatenate(
                [
                    16.0 * below[1:2] - below[0:1],
                    -below[1:2],
                    gap,
                    -above[0:1],
                    16.0 * above[0:1] - above[1:2],
                ],
                axis=0,
            )
            partial[c, z] = base[c, z] + (HALF_STEP / 12.0) * (along_z[z] + along_y)


def pack_kernel(height, spot, inner, far, plan, node, main, rest, out, near):
    column, level = spot[0] // height, spot[0] % height
    width = far.shape[0] // height

    def edge(rise, lanes):
        tiles = -(-lanes // LANES)
        rows = []
        for side in (-1, 1):
            at, up = column + side, level + rise
            inside = (at >= 0) & (at < width) & (up >= 0) & (up < height)
            source = jnp.clip(at, 0, width - 1) * height + jnp.clip(up, 0, height - 1)
            block = jnp.where(inside, far[source].astype(F32), 0.0)
            for j in range(2):
                pieces = [block[j * tiles + t : j * tiles + t + 1] for t in range(tiles)]
                rows.append(jnp.concatenate(pieces, axis=1)[:, :lanes])
        return jnp.concatenate(rows, axis=0)

    beside = edge(0, ROWS_OWN + 2 * ROWS_SLAB)
    near[...] = beside[:, :ROWS_OWN]
    edges = jnp.concatenate([beside, edge(-1, ROWS_SLAB), edge(1, ROWS_SLAB)], axis=1)
    grown = dot(edges, plan[96:100, :], TN, HIGHEST)
    cuts = (0, 320, 480, 640, 800, 960)
    parts = [grown[a:b] for a, b in zip(cuts[:-1], cuts[1:])]
    values = inner[...] + weighted_rows(parts, plan[...])
    tail = jnp.concatenate([node[2:3, :], rest[...]], axis=0)
    sphere, polar = node[0:1, :], node[1:2, :]
    coefficients = main[...]
    for s in range(out.shape[0]):
        here = jnp.where(sphere == float(s), polar, 255.0)
        block = jnp.concatenate([values, here, tail], axis=0)
        out[s, 0:16, :] = block.astype(BF16)
        out[s, 16:32, :] = coefficients


def partial_modes_kernel(arrived, radial, angular, out, rows):
    row_i = iota((NTHETA, LANES), 0).astype(F32)
    row_j = iota((NPHI, LANES), 0).astype(F32)
    dense = jnp.zeros((COMP * NTHETA, NPHI), F32)
    for s in range(0, arrived.shape[0], 2):
        left, right = [], []
        for k in (s, s + 1):
            block = arrived[k, 0:16, :].astype(F32)
            at_i = row_i == block[COMP : COMP + 1]
            at_j = row_j == block[COMP + 1 : COMP + 2]
            right.append(jnp.where(at_j, 1.0, 0.0).astype(BF16))
            left.append(
                jnp.concatenate(
                    [jnp.where(at_i, block[c : c + 1], 0.0) for c in range(COMP)], axis=0
                ).astype(BF16)
            )
        dense += dot(jnp.concatenate(left, axis=1), jnp.concatenate(right, axis=1), NT)
    exact = dense.astype(BF16)
    exact = jnp.concatenate([exact, exact], axis=1)
    for t in range(MODE_TILES):
        lanes = slice(t * LANES, (t + 1) * LANES)
        grown = dot(exact, angular[:, lanes], NN)
        weight = radial[:, lanes]
        for c in range(COMP):
            part = grown[c * NTHETA : (c + 1) * NTHETA] * weight
            rows[t * COMP + c : t * COMP + c + 1, :] = jnp.sum(part, axis=0, keepdims=True)
    sent = rows[...].astype(BF16)
    for k in range(out.shape[0]):
        out[k] = sent


def sum_modes_kernel(arrived, out):
    total = arrived[0].astype(F32)
    for k in range(1, arrived.shape[0]):
        total += arrived[k].astype(F32)
    for t in range(MODE_TILES):
        width = min(LANES, NMODE - t * LANES)
        for c in range(COMP):
            row = t * COMP + c
            out[c, :, t * LANES : t * LANES + width] = total[row : row + 1, :width]


def base_kernel(h, p, potential, coupling, section_h, out, staged, sems):
    row = iota((CY, LANES), 0)
    lane = iota((CY, LANES), 1)
    copies = []
    for c in range(COMP):
        for z in range(CZ):
            mid = h[c, z]
            staged[c, z] = mid + HALF_STEP * p[c, z]
        copy = pltpu.make_async_copy(staged.at[c], section_h.at[c], sems.at[c])
        copy.start()
        copies.append(copy)
    for c in range(COMP):
        for z in range(CZ):
            mid = h[c, z]
            total = -90.0 * mid
            for step, factor in ((1, 16.0), (2, -1.0)):
                for at in (z - step, z + step):
                    if 0 <= at < CZ:
                        total += factor * h[c, at]
                up = jnp.where(row < CY - step, pltpu.roll(mid, CY - step, 0), 0.0)
                down = jnp.where(row >= step, pltpu.roll(mid, step, 0), 0.0)
                right = jnp.where(lane < CX - step, pltpu.roll(mid, CX - step, 1), 0.0)
                left = jnp.where(lane >= step, pltpu.roll(mid, step, 1), 0.0)
                total += factor * ((up + down) + (right + left))
            coupled = coupling[c, 0] * h[0, z]
            for b in range(1, COMP):
                coupled += coupling[c, b] * h[b, z]
            out[c, z] = p[c, z] + HALF_STEP * (total * (1.0 / 12.0) - potential[z] * coupled)
    for copy in copies:
        copy.wait()


def source_kernel(
    core, patch, mine, other, high, low, series, target, partial, near_x, out, terms, sources,
    staged, sems,
):
    empty = jnp.zeros((CHEB * CHEB, LANES), BF16)
    for slot in range(SLOTS):
        chosen = patch[slot]
        first, second = mine[chosen], other[chosen]
        block = jnp.concatenate([first[16:32], second[16:32], first[0:16], second[0:16]], axis=0)
        grown = jnp.zeros((64, 2 * LANES), F32)
        for part in (high[slot], low[slot]):
            wide = jnp.concatenate(
                [jnp.concatenate([part, empty], axis=0), jnp.concatenate([empty, part], axis=0)],
                axis=1,
            )
            grown += dot(block, wide, NN)
        start = series[0, pl.ds(slot, 4, stride=SLOTS), :]
        end = series[0, pl.ds(slot + 4 * SLOTS, 4, stride=SLOTS), :]
        near = jnp.where(core[0] % 2 == 0, start, end)
        far = jnp.where(core[0] % 2 == 0, end, start)
        near, far = jnp.concatenate([near] * 4, axis=0), jnp.concatenate([far] * 4, axis=0)
        for side in range(2):
            lanes = slice(side * LANES, (side + 1) * LANES)
            main = grown[0:16, lanes] * near + grown[16:32, lanes] * far
            rest = grown[44:48, lanes] * near[0:4] + grown[60:64, lanes] * far[0:4]
            row = (slot * 2 + side) * 20
            terms[row : row + 16, :] = main
            terms[row + 16 : row + 20, :] = rest
    count = SLOTS * COMP
    total = terms[pl.ds(0, count, stride=4), :]
    for m in range(1, 4):
        total += terms[pl.ds(m, count, stride=4), :]
    sources[...] = total
    row_l = iota((CZ * CY, LANES), 0).astype(F32)
    row_x = iota((CX, LANES), 0).astype(F32)
    added = jnp.zeros((ROWS_OWN, CX), F32)
    for slot in range(0, SLOTS, 2):
        left, right = [], []
        for k in (slot, slot + 1):
            at_l = jnp.where(row_l == target[0, k : k + 1, :], 1.0, 0.0).astype(BF16)
            at_x = jnp.where(row_x == target[1, k : k + 1, :], 1.0, 0.0).astype(BF16)
            pieces = []
            for c in range(COMP):
                row = k * COMP + c
                value = jnp.broadcast_to(sources[row : row + 1, :], (16, LANES)).astype(BF16)
                pieces += [at_l[0:16] * value, at_l[16:32] * value]
            left.append(jnp.concatenate(pieces, axis=0))
            right.append(at_x)
        added += dot(jnp.concatenate(left, axis=1), jnp.concatenate(right, axis=1), NT)
    place = iota((4, LANES), 0)
    place = jnp.where(place < 2, place - 2, place + CX - 2)
    gap = jnp.abs(place - iota((4, LANES), 1))
    stencil = jnp.where(gap == 1, 16.0, jnp.where(gap == 2, -1.0, 0.0))
    added += dot(near_x[...], stencil, TN, HIGHEST) * (1.0 / 12.0)
    added = added.reshape(COMP, CZ, CY, CX)
    copies = []
    for c in range(COMP):
        staged[c] = partial[c] + HALF_STEP * added[c]
        copy = pltpu.make_async_copy(staged.at[c], out.at[c], sems.at[c])
        copy.start()
        copies.append(copy)
    for copy in copies:
        copy.wait()


def call(kernel, outs, scratch=(), smem=(), count=0, whole=(), kept=()):
    def spec(k, small=(), large=()):
        space = pltpu.SMEM if k in small else pl.ANY if k in large else pltpu.VMEM
        return pl.BlockSpec(memory_space=space)

    single = not isinstance(outs, tuple)
    results = (outs,) if single else outs
    out_specs = tuple(spec(k, large=kept) for k in range(len(results)))
    return pl.pallas_call(
        kernel,
        out_shape=outs,
        in_specs=[spec(k, smem, whole) for k in range(count)],
        out_specs=out_specs[0] if single else out_specs,
        scratch_shapes=scratch,
        name=getattr(kernel, "func", kernel).__name__,
        compiler_params=pltpu.CompilerParams(vmem_limit_bytes=VMEM_GRANT),
    )


def shape(dims, dtype=F32):
    return jax.ShapeDtypeStruct(dims, dtype)


def neighbours(axis):
    count = lax.axis_size(axis)
    forward = [(i, i + 1) for i in range(count - 1)]
    return forward, [(b, a) for a, b in forward]


def shards(
    field_h,
    field_p,
    potential,
    coupling,
    wt_cells,
    wt_coords,
    wt_patch,
    patch_coef,
    sph_points,
    sph_cells,
    sph_frac,
):
    z_count = lax.axis_size("gz")
    height = lax.axis_size("gy")
    patch = wt_patch.reshape(SLOTS)
    core = lax.axis_index(("gx", "gy")).reshape(1)
    xy_count = lax.axis_size("gx") * lax.axis_size("gy")
    up, down = neighbours("gz")
    top = field_h[:, CZ - 2 :].astype(BF16).reshape(ROWS_SLAB, LANES)
    bottom = field_h[:, :2].astype(BF16).reshape(ROWS_SLAB, LANES)
    zl = lax.ppermute(top, "gz", up)
    zh = lax.ppermute(bottom, "gz", down)
    wide, plan, node, main, rest, high, low, series, target = call(
        prep_kernel,
        (
            shape((2, CX, LANES), BF16),
            shape((104, LANES)),
            shape((3, LANES)),
            shape((16, LANES), BF16),
            shape((4, LANES)),
            shape((SLOTS, CHEB * CHEB, LANES), BF16),
            shape((SLOTS, CHEB * CHEB, LANES), BF16),
            shape((3, CHEB * SLOTS, LANES)),
            shape((2, SLOTS, LANES)),
        ),
        count=11,
        smem=(0,),
    )(
        core,
        sph_cells,
        sph_frac,
        sph_points.reshape(1, LANES),
        patch_coef[0],
        jnp.moveaxis(wt_coords[0, 0, 0], 1, 0),
        wt_cells[0, 0, 0],
        field_p,
        potential,
        coupling,
        patch,
    )
    slab = shape((ROWS_SLAB, LANES), BF16)
    pad = pltpu.VMEM((ROWS_SLAB, LANES), F32)
    cube = shape((COMP, CZ, CY, CX))
    stage = [pltpu.VMEM((COMP, CZ, CY, CX), F32), pltpu.SemaphoreType.DMA((COMP,))]
    section_h, base = call(
        base_kernel, (cube, cube), scratch=stage, count=4, smem=(3,), kept=(0,)
    )(field_h, field_p, potential, coupling)
    first, last, far = call(
        functools.partial(edges_kernel, height),
        (slab, slab, shape((xy_count, 16, LANES), BF16)),
        scratch=[pad, pad],
        count=6,
        smem=(0,),
        whole=(4, 5),
    )(core, field_h, zl, zh, base, plan)
    far = lax.all_to_all(far, ("gx", "gy"), 0, 0, tiled=True)
    up, down = neighbours("gy")
    yl = lax.ppermute(last, "gy", up)
    yh = lax.ppermute(first, "gy", down)
    grid = (field_h, zl, zh, yl, yh)
    inner, partial = call(middle_kernel, (shape((COMP, LANES)), cube), count=8)(
        *grid, wide, plan, base
    )
    packed, near_x = call(
        functools.partial(pack_kernel, height),
        (shape((z_count, SENT_ROWS, LANES), BF16), shape((4, ROWS_OWN))),
        count=7,
        smem=(0,),
    )(core, inner, far, plan, node, main, rest)
    arrived = lax.all_to_all(packed, "gz", 0, 0, tiled=True)
    partner = lax.ppermute(arrived, "gy", [(i, i ^ 1) for i in range(lax.axis_size("gy"))])
    radial, angular = mode_factors()
    sent = call(
        partial_modes_kernel,
        shape((xy_count, MODE_ROWS, LANES), BF16),
        scratch=[
            pltpu.VMEM((MODE_ROWS, LANES), F32),
        ],
        count=3,
    )(arrived, jnp.asarray(radial), jnp.asarray(angular))
    gathered = lax.all_to_all(sent, ("gx", "gy"), 0, 0, tiled=True)
    section_p = call(
        source_kernel,
        cube,
        scratch=[
            pltpu.VMEM((SLOTS * 40, LANES), F32),
            pltpu.VMEM((SLOTS * COMP, LANES), F32),
            *stage,
        ],
        count=10,
        smem=(0, 1),
        kept=(0,),
    )(
        core,
        patch,
        arrived,
        partner,
        high,
        low,
        series,
        target,
        partial,
        near_x,
    )
    modes = call(sum_modes_kernel, shape((COMP, 1, NMODE)), count=1)(gathered)
    return section_h, section_p, jnp.moveaxis(modes, 1, 0)


def solution(mesh):
    placed = (
        P(None, "gz", "gy", "gx"),
        P(None, "gz", "gy", "gx"),
        P("gz", "gy", "gx"),
        P(),
        P("gz", "gy", "gx", None, None),
        P("gz", "gy", "gx", None, None, None),
        P("gz", "gy", "gx", None, None),
        P("gz", None, None, None),
        P(("gx", "gy", "gz")),
        P(None, ("gx", "gy", "gz")),
        P(None, ("gx", "gy", "gz")),
    )
    return jax.shard_map(
        shards,
        mesh=mesh,
        in_specs=placed,
        out_specs=(P(None, "gz", "gy", "gx"), P(None, "gz", "gy", "gx"), P("gz", None, None)),
        check_vma=False,
    )
```

time: 80.9 us -> 74.2 us (0.917)
  blocking collectives: 33.9 us -> 28.3 us
  starting transfers between devices: 28.9 us -> 25.6 us
  waiting for transfers between devices: 5.6 us -> 7.91 us
  local copies, waits for them, and re-layouts: 3.03 us -> 1.35 us
  other arithmetic: 0 us -> 0.98 us
    all_to_all x0 -> x1, starting transfers between devices: none -> 7.15 us  [shards(): far = lax.all_to_all(far, ('gx', 'gy'), 0, 0, tiled=True)]
    all_to_all x1, blocking collectives: 33.9 us -> 28.3 us  [shards(): arrived = lax.all_to_all(packed, 'gz', 0, 0, tiled=True)]
    ppermute x4 -> x2, starting transfers between devices: 11.2 us -> 6.11 us  [the longest x1 4.82 us: shards(): zl = lax.ppermute(top, 'gz', up)]
    ppermute x1, starting transfers between devices: 5.1 us -> 1.92 us  [shards(): yh = lax.ppermute(first, 'gy', down)]
    ppermute x4 -> x2, waiting for transfers between devices: 3.27 us -> 0.84 us  [the longest x1 0.83 us: shards(): zh = lax.ppermute(bottom, 'gz', down)]
    ppermute x1, waiting for transfers between devices: 1 us -> 3.38 us  [shards(): yh = lax.ppermute(first, 'gy', down)]
    ppermute x1, waiting for transfers between devices: 0.01 us -> 1.4 us  [shards(): lax.ppermute(arrived, 'gy', [(i, i ^ 1) for i in range(lax.axis_size('gy'...]
    ppermute x1, starting transfers between devices: 4.62 us -> 3.53 us  [shards(): yl = lax.ppermute(last, 'gy', up)]
  transfers between devices with their start and end apart: 8 -> 7, of which waited for: 4 -> 4; matrix products, arithmetic and copies ran while one was open for 0% -> 0% of each run, Pallas kernels for 5% -> 6%
where the time goes in v3:
time: 74.2 us; the launch traced here: 73.7 us
  blocking collectives  28.3 us (38%)
  starting transfers between devices  25.6 us (35%)
  Pallas kernels  8.6 us (12%)
  waiting for transfers between devices  7.91 us (11%)
  local copies, waits for them, and re-layouts  1.35 us (2%)
  other arithmetic  0.98 us (1%)
  between operations  0.88 us (1%)
    all_to_all x1, blocking collectives, shards(): arrived = lax.all_to_all(packed, 'gz', 0, 0, tiled=True)  28.3 us
    all_to_all x1, starting transfers between devices, shards(): far = lax.all_to_all(far, ('gx', 'gy'), 0, 0, tiled=True)  7.15 us
    all_to_all x1, starting transfers between devices, shards(): gathered = lax.all_to_all(sent, ('gx', 'gy'), 0, 0, tiled=True)  4.9 us
    ppermute x1, starting transfers between devices, shards(): zl = lax.ppermute(top, 'gz', up)  4.82 us
    ppermute x1, starting transfers between devices, shards(): yl = lax.ppermute(last, 'gy', up)  3.53 us
    ppermute x1, waiting for transfers between devices, shards(): yh = lax.ppermute(first, 'gy', down)  3.38 us
    all_to_all x1, waiting for transfers between devices, shards(): gathered = lax.all_to_all(sent, ('gx', 'gy'), 0, 0, tiled=True)  2.29 us
    pallas_call x1, Pallas kernels, shards(): call(partial_modes_kernel, shape((xy_count, MODE_ROWS, LANES), BF16), scr...  2.23 us
  transfers between devices with their start and end apart: 7, of which 4 were waited for; matrix products, arithmetic and copies ran while one was open for 0% of the time, Pallas kernels for 6%

profile of v3, /device:TPU:1, one launch (start us, length us, event | category | flops | bytes accessed | tf_op | source)
XLA Modules:
  0.0 73.7 jit_solution(587347352961622371)
XLA Ops:
  0.6 1.0 %convert.4 = bf16[10,4,8,128]{3,2,1,0:T(8,128)(2,1)S(1)} convert(f32[10,4,8,128]{3,2,1,0:T(8,128)} %h.5) | non-fusion elementwise | flops 40960 | bytes 245760 | tf_op jit(solution)/shard_map/convert.1
  1.7 0.0 copy-start.4
  1.7 4.8 %collective-permute-start = (bf16[160,128]{1,0:T(8,128)(2,1)S(1)}, bf16[160,128]{1,0:T(8,128)(2,1)S(1)}, u32[]{:S(2)}, u32[]{:S(2)}) collective-permute-start(bf16[160,128]{1,0:T(8,128)(2,1)S(1)} %bitcast.18), channel_id=1, source_target_pairs={{0,1},{1,2},{2,3},{3,4},{4,5},{5,6},{6,7},{7,8},{8,9},{9,10},{10,1... | collective-permute-start | bytes 122888 | tf_op jit(solution)/shard_map/ppermute | solution.py:464
  6.5 1.3 %collective-permute-start.1 = (bf16[160,128]{1,0:T(8,128)(2,1)S(1)}, bf16[160,128]{1,0:T(8,128)(2,1)S(1)}, u32[]{:S(2)}, u32[]{:S(2)}) collective-permute-start(bf16[160,128]{1,0:T(8,128)(2,1)S(1)} %bitcast.17), channel_id=1, source_target_pairs={{1,0},{2,1},{3,2},{4,3},{5,4},{6,5},{7,6},{8,7},{9,8},{10,9},{11,1... | collective-permute-start | bytes 122888 | tf_op jit(solution)/shard_map/ppermute | solution.py:465
  7.8 0.0 copy-start.6
  7.8 0.7 copy-done.6
  8.5 1.7 %base_kernel.1 = (f32[10,4,8,128]{3,2,1,0:T(8,128)}, f32[10,4,8,128]{3,2,1,0:T(8,128)S(1)}) custom-call(f32[10,4,8,128]{3,2,1,0:T(8,128)S(1)} %copy-done, f32[10,4,8,128]{3,2,1,0:T(8,128)S(1)} %copy-done.1, f32[4,8,128]{2,1,0:T(8,128)S(1)} %copy-done.4, f32[10,10]{1,0:T(8,128)S(1)} %copy-done.6), custom_call_target="tpu_custom_call" | custom-call | tf_op jit(solution)/shard_map/base_kernel/pallas_call | solution.py:498
  10.2 0.0 copy-start.8
  10.2 0.0 copy-start.9
  10.2 0.0 copy-start.11
  10.2 0.0 copy-start.12
  10.3 0.6 copy-done.8
  10.9 0.0 copy-done.9
  10.9 0.1 prep_kernel.1
  11.0 0.8 %collective-permute-done.1.zh = bf16[160,128]{1,0:T(8,128)(2,1)S(1)} collective-permute-done((bf16[160,128]{1,0:T(8,128)(2,1)S(1)}, bf16[160,128]{1,0:T(8,128)(2,1)S(1)}, u32[]{:S(2)}, u32[]{:S(2)}) %collective-permute-start.1) | collective-permute-done | bytes 40992 | tf_op jit(solution)/shard_map/ppermute | solution.py:465
  11.9 0.9 %edges_kernel.1 = (bf16[160,128]{1,0:T(8,128)(2,1)S(1)}, bf16[160,128]{1,0:T(8,128)(2,1)S(1)}, bf16[16,16,128]{2,1,0:T(8,128)(2,1)}) custom-call(s32[1]{0:T(128)} %bitcast.core.spot, f32[10,4,8,128]{3,2,1,0:T(8,128)S(1)} %copy-done, bf16[160,128]{1,0:T(8,128)(2,1)S(1)} %collective-permute-done.zl, bf16[160,128]{1,0:T(8,128)(2,1)S(1)} %collective-permute-done.1.zh, ...), custom_call_target="tpu_custom_call" | custom-call | tf_op jit(solution)/shard_map/edges_kernel/pallas_call | solution.py:501
  12.8 7.1 %all-to-all-start = ((bf16[16,16,128]{2,1,0:T(8,128)(2,1)}), bf16[16,16,128]{2,1,0:T(8,128)(2,1)S(1)}, u32[]{:S(2)}, u32[]{:S(2)}) async-start(bf16[16,16,128]{2,1,0:T(8,128)(2,1)} %get-tuple-element.28), calls=%async_computation | async-start | bytes 131072 | tf_op jit(solution)/shard_map/all_to_all | solution.py:509
  19.9 3.5 %collective-permute-start.2 = (bf16[160,128]{1,0:T(8,128)(2,1)S(1)}, bf16[160,128]{1,0:T(8,128)(2,1)S(1)}, u32[]{:S(2)}, u32[]{:S(2)}) collective-permute-start(bf16[160,128]{1,0:T(8,128)(2,1)S(1)} %get-tuple-element.24), channel_id=1, source_target_pairs={{0,32},{32,64},{64,96},{1,33},{33,65},{65,97},{2,34},{34,66},{66,9... | collective-permute-start | bytes 122888 | tf_op jit(solution)/shard_map/ppermute | solution.py:511
  23.5 1.9 %collective-permute-start.3 = (bf16[160,128]{1,0:T(8,128)(2,1)S(1)}, bf16[160,128]{1,0:T(8,128)(2,1)S(1)}, u32[]{:S(2)}, u32[]{:S(2)}) collective-permute-start(bf16[160,128]{1,0:T(8,128)(2,1)S(1)} %get-tuple-element.25), channel_id=1, source_target_pairs={{32,0},{64,32},{96,64},{33,1},{65,33},{97,65},{34,2},{66,34},{98,6... | collective-permute-start | bytes 122888 | tf_op jit(solution)/shard_map/ppermute | solution.py:512
  25.4 3.4 %collective-permute-done.3.yh = bf16[160,128]{1,0:T(8,128)(2,1)S(1)} collective-permute-done((bf16[160,128]{1,0:T(8,128)(2,1)S(1)}, bf16[160,128]{1,0:T(8,128)(2,1)S(1)}, u32[]{:S(2)}, u32[]{:S(2)}) %collective-permute-start.3) | collective-permute-done | bytes 40992 | tf_op jit(solution)/shard_map/ppermute | solution.py:512
  28.8 0.3 middle_kernel.1
  29.2 0.7 pack_kernel.1
  29.8 0.0 copy-start.2
  29.8 0.0 copy-start.3
  29.8 28.3 %all_to_all.15.mine.arrived = bf16[32,32,128]{2,1,0:T(8,128)(2,1)S(1)} all-to-all(bf16[32,32,128]{2,1,0:T(8,128)(2,1)S(1)} %get-tuple-element.32), channel_id=1, replica_groups=mesh['gx'=4,'gy'=4,'gz'=32] {'gz'}, dimensions={0} | all-to-all | bytes 524288 | tf_op jit(solution)/shard_map/all_to_all | solution.py:523
  58.2 2.2 %partial_modes_kernel.1 = bf16[16,80,128]{2,1,0:T(8,128)(2,1)} custom-call(bf16[32,32,128]{2,1,0:T(8,128)(2,1)S(1)} %all_to_all.15.mine.arrived, f32[32,1024]{1,0:T(8,128)S(1)} %copy-done.3, bf16[128,1024]{1,0:T(8,128)(2,1)S(1)} %copy-done.2), custom_call_target="tpu_custom_call" | custom-call | tf_op jit(solution)/shard_map/partial_modes_kernel/pallas_call | solution.py:526
  60.4 4.9 %all-to-all-start.2 = ((bf16[16,80,128]{2,1,0:T(8,128)(2,1)}), bf16[16,80,128]{2,1,0:T(8,128)(2,1)S(1)}, u32[]{:S(2)}, u32[]{:S(2)}) async-start(bf16[16,80,128]{2,1,0:T(8,128)(2,1)} %partial_modes_kernel.1), calls=%async_computation.2 | async-start | bytes 655360 | tf_op jit(solution)/shard_map/all_to_all | solution.py:534
  65.3 2.0 %collective-permute-start.4 = (bf16[32,32,128]{2,1,0:T(8,128)(2,1)S(1)}, bf16[32,32,128]{2,1,0:T(8,128)(2,1)S(1)}, u32[]{:S(2)}, u32[]{:S(2)}) collective-permute-start(bf16[32,32,128]{2,1,0:T(8,128)(2,1)S(1)} %all_to_all.15.mine.arrived), channel_id=1, source_target_pairs={{0,32},{32,0},{64,96},{96,64},{1,33},{33,1},{65,97},{97,65},{2,34}... | collective-permute-start | bytes 786440 | tf_op jit(solution)/shard_map/ppermute | solution.py:524
  67.3 1.4 %collective-permute-done.4.other = bf16[32,32,128]{2,1,0:T(8,128)(2,1)S(1)} collective-permute-done((bf16[32,32,128]{2,1,0:T(8,128)(2,1)S(1)}, bf16[32,32,128]{2,1,0:T(8,128)(2,1)S(1)}, u32[]{:S(2)}, u32[]{:S(2)}) %collective-permute-start.4) | collective-permute-done | bytes 262176 | tf_op jit(solution)/shard_map/ppermute | solution.py:524
  68.7 2.0 %source_kernel.1 = f32[10,4,8,128]{3,2,1,0:T(8,128)} custom-call(s32[1]{0:T(128)} %bitcast.core.spot, s32[8]{0:T(128)S(1)} %bitcast.15, bf16[32,32,128]{2,1,0:T(8,128)(2,1)S(1)} %all_to_all.15.mine.arrived, bf16[32,32,128]{2,1,0:T(8,128)(2,1)S(1)} %collective-permute-done.4.other, bf16[8,64,128]{2,1,0:T(8,128)(2,1)S(1)} %get-tuple-element.33.high, ...), custom_call_target="tpu_custom_call" | custom-call | tf_op jit(solution)/shard_map/source_kernel/pallas_call | solution.py:535
  70.7 2.3 %all-to-all-done.2.arrived = bf16[16,80,128]{2,1,0:T(8,128)(2,1)S(1)} async-done(((bf16[16,80,128]{2,1,0:T(8,128)(2,1)}), bf16[16,80,128]{2,1,0:T(8,128)(2,1)S(1)}, u32[]{:S(2)}, u32[]{:S(2)}) %all-to-all-start.2) | async-done | bytes 327712 | tf_op jit(solution)/shard_map/all_to_all | solution.py:534
  73.0 0.7 sum_modes_kernel.1
  (19 shorter events, 0.0 us)
Async XLA Ops:
  0.6 7.2 %copy-start = (f32[10,4,8,128]{3,2,1,0:T(8,128)S(1)}, f32[10,4,8,128]{3,2,1,0:T(8,128)}, u32[]{:S(2)}) copy-start(f32[10,4,8,128]{3,2,1,0:T(8,128)} %h.5) | copy-start | bytes 491524
  0.6 7.2 %copy-start.1 = (f32[10,4,8,128]{3,2,1,0:T(8,128)S(1)}, f32[10,4,8,128]{3,2,1,0:T(8,128)}, u32[]{:S(2)}) copy-start(f32[10,4,8,128]{3,2,1,0:T(8,128)} %p.3) | copy-start | bytes 491524
  1.7 6.2 %copy-start.4 = (f32[4,8,128]{2,1,0:T(8,128)S(1)}, f32[4,8,128]{2,1,0:T(8,128)}, u32[]{:S(2)}) copy-start(f32[4,8,128]{2,1,0:T(8,128)} %v.1) | copy-start | bytes 49156
  1.7 9.4 %collective-permute-start = (bf16[160,128]{1,0:T(8,128)(2,1)S(1)}, bf16[160,128]{1,0:T(8,128)(2,1)S(1)}, u32[]{:S(2)}, u32[]{:S(2)}) collective-permute-start(bf16[160,128]{1,0:T(8,128)(2,1)S(1)} %bitcast.18), channel_id=1, source_target_pairs={{0,1},{1,2},{2,3},{3,4},{4,5},{5,6},{6,7},{7,8},{8,9},{9,10},{10,1... | collective-permute-start | bytes 122888 | tf_op jit(solution)/shard_map/ppermute | solution.py:464
  6.5 5.4 %collective-permute-start.1 = (bf16[160,128]{1,0:T(8,128)(2,1)S(1)}, bf16[160,128]{1,0:T(8,128)(2,1)S(1)}, u32[]{:S(2)}, u32[]{:S(2)}) collective-permute-start(bf16[160,128]{1,0:T(8,128)(2,1)S(1)} %bitcast.17), channel_id=1, source_target_pairs={{1,0},{2,1},{3,2},{4,3},{5,4},{6,5},{7,6},{8,7},{9,8},{10,9},{11,1... | collective-permute-start | bytes 122888 | tf_op jit(solution)/shard_map/ppermute | solution.py:465
  7.8 0.7 copy-start.6
  8.5 1.8 %copy-start.5 = (f32[1,10,8,64]{3,2,1,0:T(8,128)S(1)}, f32[1,10,8,64]{3,2,1,0:T(8,128)}, u32[]{:S(2)}) copy-start(f32[1,10,8,64]{3,2,1,0:T(8,128)} %param.20) | copy-start | bytes 61444
  8.5 1.8 %copy-start.7 = (f32[1,1,1,8,3,128]{5,3,4,2,1,0:T(8,128)S(1)}, f32[1,1,1,8,3,128]{5,3,4,2,1,0:T(8,128)}, u32[]{:S(2)}) copy-start(f32[1,1,1,8,3,128]{5,3,4,2,1,0:T(8,128)} %param.18) | copy-start | bytes 36868
  8.5 1.8 %copy-start.10 = (f32[3,128]{1,0:T(4,128)S(1)}, f32[3,128]{1,0:T(4,128)}, u32[]{:S(2)}) copy-start(f32[3,128]{1,0:T(4,128)} %frac.1) | copy-start | bytes 4612
  10.2 0.7 copy-start.8
  10.2 0.7 copy-start.9
  10.2 0.7 copy-start.11
  10.2 0.7 copy-start.12
  12.8 16.4 %all-to-all-start = ((bf16[16,16,128]{2,1,0:T(8,128)(2,1)}), bf16[16,16,128]{2,1,0:T(8,128)(2,1)S(1)}, u32[]{:S(2)}, u32[]{:S(2)}) async-start(bf16[16,16,128]{2,1,0:T(8,128)(2,1)} %get-tuple-element.28), calls=%async_computation | async-start | bytes 131072 | tf_op jit(solution)/shard_map/all_to_all | solution.py:509
  19.9 5.5 %collective-permute-start.2 = (bf16[160,128]{1,0:T(8,128)(2,1)S(1)}, bf16[160,128]{1,0:T(8,128)(2,1)S(1)}, u32[]{:S(2)}, u32[]{:S(2)}) collective-permute-start(bf16[160,128]{1,0:T(8,128)(2,1)S(1)} %get-tuple-element.24), channel_id=1, source_target_pairs={{0,32},{32,64},{64,96},{1,33},{33,65},{65,97},{2,34},{34,66},{66,9... | collective-permute-start | bytes 122888 | tf_op jit(solution)/shard_map/ppermute | solution.py:511
  23.5 5.3 %collective-permute-start.3 = (bf16[160,128]{1,0:T(8,128)(2,1)S(1)}, bf16[160,128]{1,0:T(8,128)(2,1)S(1)}, u32[]{:S(2)}, u32[]{:S(2)}) collective-permute-start(bf16[160,128]{1,0:T(8,128)(2,1)S(1)} %get-tuple-element.25), channel_id=1, source_target_pairs={{32,0},{64,32},{96,64},{33,1},{65,33},{97,65},{34,2},{66,34},{98,6... | collective-permute-start | bytes 122888 | tf_op jit(solution)/shard_map/ppermute | solution.py:512
  29.8 28.3 %copy-start.2 = (bf16[128,1024]{1,0:T(8,128)(2,1)S(1)}, bf16[128,1024]{1,0:T(8,128)(2,1)}, u32[]{:S(2)}) copy-start(bf16[128,1024]{1,0:T(8,128)(2,1)} %constant.17.clone.angular) | copy-start | bytes 786436
  29.8 28.3 %copy-start.3 = (f32[32,1024]{1,0:T(8,128)S(1)}, f32[32,1024]{1,0:T(8,128)}, u32[]{:S(2)}) copy-start(f32[32,1024]{1,0:T(8,128)} %constant.16.clone.radial) | copy-start | bytes 393220
  60.4 12.6 %all-to-all-start.2 = ((bf16[16,80,128]{2,1,0:T(8,128)(2,1)}), bf16[16,80,128]{2,1,0:T(8,128)(2,1)S(1)}, u32[]{:S(2)}, u32[]{:S(2)}) async-start(bf16[16,80,128]{2,1,0:T(8,128)(2,1)} %partial_modes_kernel.1), calls=%async_computation.2 | async-start | bytes 655360 | tf_op jit(solution)/shard_map/all_to_all | solution.py:534
  65.3 3.4 %collective-permute-start.4 = (bf16[32,32,128]{2,1,0:T(8,128)(2,1)S(1)}, bf16[32,32,128]{2,1,0:T(8,128)(2,1)S(1)}, u32[]{:S(2)}, u32[]{:S(2)}) collective-permute-start(bf16[32,32,128]{2,1,0:T(8,128)(2,1)S(1)} %all_to_all.15.mine.arrived), channel_id=1, source_target_pairs={{0,32},{32,0},{64,96},{96,64},{1,33},{33,1},{65,97},{97,65},{2,34}... | collective-permute-start | bytes 786440 | tf_op jit(solution)/shard_map/ppermute | solution.py:524

commit v4 on v3

--- a/solution.py
+++ b/solution.py
@@ -31,6 +31,7 @@
 SENT_ROWS = 32
 SLOTS = 8
 VMEM_GRANT = 8 << 20
+PLANE = 64
 
 F32 = jnp.float32
 BF16 = jnp.bfloat16
@@ -112,6 +113,10 @@
             total += yh[base : base + 8] * plan[80 + z * 8 : 88 + z * 8]
         rows.append(jnp.sum(total, axis=0, keepdims=True))
     return jnp.concatenate(rows, axis=0)
+
+
+def low_high(even, first, second):
+    return jnp.where(even, second, first), jnp.where(even, first, second)
 
 
 def prep_kernel(
@@ -163,8 +168,9 @@
     target[1] = (cell % CX).astype(F32)
 
 
-def edges_kernel(height, spot, h, zl, zh, base, plan, first, last, far, lower, upper):
-    low, high = zl[...].astype(F32), zh[...].astype(F32)
+def edges_kernel(height, spot, h, za, zb, base, plan, first, last, far, lower, upper):
+    zl, zh = za[...], zb[...]
+    low, high = zl.astype(F32), zh.astype(F32)
     for c in range(COMP):
         for z in range(CZ + 4):
             if z < 2:
@@ -177,14 +183,13 @@
             lower[row : row + 2, :] = source[0:2]
             upper[row : row + 2, :] = source[CY - 2 : CY]
     below, above = lower[...].astype(BF16), upper[...].astype(BF16)
-    first[...] = below
-    last[...] = above
+    last[...], first[...] = low_high(spot[0] % 2 == 0, above, below)
     row = iota((8, LANES), 0)
     lane = iota((8, LANES), 1)
     place = jnp.where(row < 2, row, row + CX - 4)
     pick = jnp.where(lane == place, 1.0, 0.0).astype(BF16)
     own = h[...].reshape(ROWS_OWN, LANES).astype(BF16)
-    wide = jnp.concatenate([dot(pick, part, NT) for part in (own, zl[...], zh[...])], axis=1)
+    wide = jnp.concatenate([dot(pick, part, NT) for part in (own, zl, zh)], axis=1)
     empty = jnp.zeros((8, 2 * LANES - ROWS_SLAB), F32)
 
     def block(edge, start):
@@ -200,7 +205,7 @@
     below = jnp.concatenate([dot(pick, below, NT), empty], axis=1)
     above = jnp.concatenate([dot(pick, above, NT), empty], axis=1)
     blocks = [[block(edge, start) for start in (0, 2)] for edge in (wide, below, above)]
-    column, level = spot[0] // height, spot[0] % height
+    column, level = spot[0] % PLANE // height, spot[0] % height
     for e in range(far.shape[0]):
         right = e // height == column + 1
         inner, lower_row, upper_row = [jnp.where(right, hi, lo) for lo, hi in blocks]
@@ -208,14 +213,16 @@
         far[e] = jnp.where(e % height == level, inner, outer)
 
 
-def middle_kernel(h, zl, zh, yl, yh, wide, plan, base, out, partial):
+def middle_kernel(spot, h, za, zb, ya, yb, wide, plan, base, out, partial):
+    zl, zh = za[...], zb[...]
+    yl, yh = low_high(spot[0] % 2 == 0, ya[...], yb[...])
     high, low = split2(h[...].reshape(ROWS_OWN, LANES))
     near, fine = wide[0], wide[1]
     parts = [dot(high, near, NN) + dot(low, near, NN) + dot(high, fine, NN)]
-    parts += [dot(slab[...], near, NN) + dot(slab[...], fine, NN) for slab in (zl, zh, yl, yh)]
+    parts += [dot(slab, near, NN) + dot(slab, fine, NN) for slab in (zl, zh, yl, yh)]
     out[...] = weighted_rows(parts, plan[...])
-    z_low, z_high = zl[...].astype(F32), zh[...].astype(F32)
-    y_low, y_high = yl[...].astype(F32), yh[...].astype(F32)
+    z_low, z_high = zl.astype(F32), zh.astype(F32)
+    y_low, y_high = yl.astype(F32), yh.astype(F32)
     gap = jnp.zeros((CY - 4, LANES), F32)
     for c in range(COMP):
         at = c * 2 * CY
@@ -239,7 +246,7 @@
 
 
 def pack_kernel(height, spot, inner, far, plan, node, main, rest, out, near):
-    column, level = spot[0] // height, spot[0] % height
+    column, level = spot[0] % PLANE // height, spot[0] % height
     width = far.shape[0] // height
 
     def edge(rise, lanes):
@@ -434,6 +441,13 @@
     return jax.ShapeDtypeStruct(dims, dtype)
 
 
+def exchanges(axis):
+    count = lax.axis_size(axis)
+    near = [(i, i ^ 1) for i in range(count)]
+    upward = [(i, i + 1) for i in range(1, count - 1, 2)]
+    return near, upward + [(b, a) for a, b in upward]
+
+
 def neighbours(axis):
     count = lax.axis_size(axis)
     forward = [(i, i + 1) for i in range(count - 1)]
@@ -456,13 +470,14 @@
     z_count = lax.axis_size("gz")
     height = lax.axis_size("gy")
     patch = wt_patch.reshape(SLOTS)
-    core = lax.axis_index(("gx", "gy")).reshape(1)
+    even = lax.axis_index("gz") % 2 == 0
+    core = (lax.axis_index(("gx", "gy")) + jnp.where(even, 0, PLANE)).reshape(1)
     xy_count = lax.axis_size("gx") * lax.axis_size("gy")
-    up, down = neighbours("gz")
+    near, far = neighbours("gz")
     top = field_h[:, CZ - 2 :].astype(BF16).reshape(ROWS_SLAB, LANES)
     bottom = field_h[:, :2].astype(BF16).reshape(ROWS_SLAB, LANES)
-    zl = lax.ppermute(top, "gz", up)
-    zh = lax.ppermute(bottom, "gz", down)
+    za = lax.ppermute(top, "gz", near)
+    zb = lax.ppermute(bottom, "gz", far)
     wide, plan, node, main, rest, high, low, series, target = call(
         prep_kernel,
         (
@@ -505,15 +520,14 @@
         count=6,
         smem=(0,),
         whole=(4, 5),
-    )(core, field_h, zl, zh, base, plan)
+    )(core, field_h, za, zb, base, plan)
     far = lax.all_to_all(far, ("gx", "gy"), 0, 0, tiled=True)
-    up, down = neighbours("gy")
-    yl = lax.ppermute(last, "gy", up)
-    yh = lax.ppermute(first, "gy", down)
-    grid = (field_h, zl, zh, yl, yh)
-    inner, partial = call(middle_kernel, (shape((COMP, LANES)), cube), count=8)(
-        *grid, wide, plan, base
-    )
+    near, distant = exchanges("gy")
+    ya = lax.ppermute(first, "gy", near)
+    yb = lax.ppermute(last, "gy", distant)
+    inner, partial = call(
+        middle_kernel, (shape((COMP, LANES)), cube), count=9, smem=(0,)
+    )(core, field_h, za, zb, ya, yb, wide, plan, base)
     packed, near_x = call(
         functools.partial(pack_kernel, height),
         (shape((z_count, SENT_ROWS, LANES), BF16), shape((4, ROWS_OWN))),

time: 74.2 us -> 74 us (level)
  waiting for transfers between devices: 7.91 us -> 6.35 us
  starting transfers between devices: 25.6 us -> 27 us
    ppermute x4, waiting for transfers between devices: 4.22 us -> 2.65 us  [the longest x1 1.84 us: shards(): yb = lax.ppermute(last, 'gy', distant)]
    all_to_all x1, starting transfers between devices: 4.9 us -> 6.03 us  [shards(): gathered = lax.all_to_all(sent, ('gx', 'gy'), 0, 0, tiled=True)]
where the time goes in v4:
time: 74 us; the launch traced here: 73.5 us
  blocking collectives  28.3 us (38%)
  starting transfers between devices  27 us (36%)
  Pallas kernels  8.6 us (12%)
  waiting for transfers between devices  6.35 us (9%)
  local copies, waits for them, and re-layouts  1.36 us (2%)
  other arithmetic  0.97 us (1%)
  between operations  0.89 us (1%)
    all_to_all x1, blocking collectives, shards(): arrived = lax.all_to_all(packed, 'gz', 0, 0, tiled=True)  28.3 us
    all_to_all x1, starting transfers between devices, shards(): far = lax.all_to_all(far, ('gx', 'gy'), 0, 0, tiled=True)  7.15 us
    all_to_all x1, starting transfers between devices, shards(): gathered = lax.all_to_all(sent, ('gx', 'gy'), 0, 0, tiled=True)  6.03 us
    ppermute x1, starting transfers between devices, shards(): za = lax.ppermute(top, 'gz', near)  4.95 us
    ppermute x1, starting transfers between devices, shards(): yb = lax.ppermute(last, 'gy', distant)  3.46 us
    all_to_all x1, waiting for transfers between devices, shards(): gathered = lax.all_to_all(sent, ('gx', 'gy'), 0, 0, tiled=True)  2.3 us
    pallas_call x1, Pallas kernels, shards(): call(partial_modes_kernel, shape((xy_count, MODE_ROWS, LANES), BF16), scr...  2.23 us
    ppermute x1, starting transfers between devices, shards(): ya = lax.ppermute(first, 'gy', near)  2.09 us
  transfers between devices with their start and end apart: 7, of which 4 were waited for; matrix products, arithmetic and copies ran while one was open for 0% of the time, Pallas kernels for 6%

profile of v4, /device:TPU:1, one launch (start us, length us, event | category | flops | bytes accessed | tf_op | source)
XLA Modules:
  0.0 73.5 jit_solution(2416910491355426746)
XLA Ops:
  0.6 1.0 %convert.4 = bf16[10,4,8,128]{3,2,1,0:T(8,128)(2,1)S(1)} convert(f32[10,4,8,128]{3,2,1,0:T(8,128)} %h.5) | non-fusion elementwise | flops 40960 | bytes 245760 | tf_op jit(solution)/shard_map/convert.1
  1.6 0.0 copy-start
  1.6 4.9 %collective-permute-start = (bf16[160,128]{1,0:T(8,128)(2,1)S(1)}, bf16[160,128]{1,0:T(8,128)(2,1)S(1)}, u32[]{:S(2)}, u32[]{:S(2)}) collective-permute-start(bf16[160,128]{1,0:T(8,128)(2,1)S(1)} %bitcast.18), channel_id=1, source_target_pairs={{0,1},{1,2},{2,3},{3,4},{4,5},{5,6},{6,7},{7,8},{8,9},{9,10},{10,1... | collective-permute-start | bytes 122888 | tf_op jit(solution)/shard_map/ppermute | solution.py:479
  6.6 1.3 %collective-permute-start.1 = (bf16[160,128]{1,0:T(8,128)(2,1)S(1)}, bf16[160,128]{1,0:T(8,128)(2,1)S(1)}, u32[]{:S(2)}, u32[]{:S(2)}) collective-permute-start(bf16[160,128]{1,0:T(8,128)(2,1)S(1)} %bitcast.17), channel_id=1, source_target_pairs={{1,0},{2,1},{3,2},{4,3},{5,4},{6,5},{7,6},{8,7},{9,8},{10,9},{11,1... | collective-permute-start | bytes 122888 | tf_op jit(solution)/shard_map/ppermute | solution.py:480
  7.9 0.0 copy-start.4
  7.9 0.0 copy-start.6
  8.0 0.7 copy-done.4
  8.6 1.7 %base_kernel.1 = (f32[10,4,8,128]{3,2,1,0:T(8,128)}, f32[10,4,8,128]{3,2,1,0:T(8,128)S(1)}) custom-call(f32[10,4,8,128]{3,2,1,0:T(8,128)S(1)} %copy-done, f32[10,4,8,128]{3,2,1,0:T(8,128)S(1)} %copy-done.1, f32[4,8,128]{2,1,0:T(8,128)S(1)} %copy-done.4, f32[10,10]{1,0:T(8,128)S(1)} %copy-done.6), custom_call_target="tpu_custom_call" | custom-call | tf_op jit(solution)/shard_map/base_kernel/pallas_call | solution.py:513
  10.3 0.0 copy-start.8
  10.4 0.0 copy-start.9
  10.4 0.0 copy-start.12
  10.4 0.6 copy-done.8
  11.0 0.0 copy-done.9
  11.0 0.1 prep_kernel.1
  11.2 0.8 %collective-permute-done.1.zb = bf16[160,128]{1,0:T(8,128)(2,1)S(1)} collective-permute-done((bf16[160,128]{1,0:T(8,128)(2,1)S(1)}, bf16[160,128]{1,0:T(8,128)(2,1)S(1)}, u32[]{:S(2)}, u32[]{:S(2)}) %collective-permute-start.1) | collective-permute-done | bytes 40992 | tf_op jit(solution)/shard_map/ppermute | solution.py:480
  12.0 0.9 %edges_kernel.1 = (bf16[160,128]{1,0:T(8,128)(2,1)S(1)}, bf16[160,128]{1,0:T(8,128)(2,1)S(1)}, bf16[16,16,128]{2,1,0:T(8,128)(2,1)}) custom-call(s32[1]{0:T(128)} %bitcast.core.spot, f32[10,4,8,128]{3,2,1,0:T(8,128)S(1)} %copy-done, bf16[160,128]{1,0:T(8,128)(2,1)S(1)} %collective-permute-done.za, bf16[160,128]{1,0:T(8,128)(2,1)S(1)} %collective-permute-done.1.zb, ...), custom_call_target="tpu_custom_call" | custom-call | tf_op jit(solution)/shard_map/edges_kernel/pallas_call | solution.py:516
  12.9 7.1 %all-to-all-start = ((bf16[16,16,128]{2,1,0:T(8,128)(2,1)}), bf16[16,16,128]{2,1,0:T(8,128)(2,1)S(1)}, u32[]{:S(2)}, u32[]{:S(2)}) async-start(bf16[16,16,128]{2,1,0:T(8,128)(2,1)} %get-tuple-element.28), calls=%async_computation | async-start | bytes 131072 | tf_op jit(solution)/shard_map/all_to_all | solution.py:524
  20.1 2.1 %collective-permute-start.2 = (bf16[160,128]{1,0:T(8,128)(2,1)S(1)}, bf16[160,128]{1,0:T(8,128)(2,1)S(1)}, u32[]{:S(2)}, u32[]{:S(2)}) collective-permute-start(bf16[160,128]{1,0:T(8,128)(2,1)S(1)} %get-tuple-element.24), channel_id=1, source_target_pairs={{0,32},{32,0},{64,96},{96,64},{1,33},{33,1},{65,97},{97,65},{2,34}... | collective-permute-start | bytes 122888 | tf_op jit(solution)/shard_map/ppermute | solution.py:526
  22.2 3.5 %collective-permute-start.3 = (bf16[160,128]{1,0:T(8,128)(2,1)S(1)}, bf16[160,128]{1,0:T(8,128)(2,1)S(1)}, u32[]{:S(2)}, u32[]{:S(2)}) collective-permute-start(bf16[160,128]{1,0:T(8,128)(2,1)S(1)} %get-tuple-element.25), channel_id=1, source_target_pairs={{32,64},{64,32},{33,65},{65,33},{34,66},{66,34},{35,67},{67,35},{3... | collective-permute-start | bytes 122888 | tf_op jit(solution)/shard_map/ppermute | solution.py:527
  25.6 1.8 %collective-permute-done.3.yb = bf16[160,128]{1,0:T(8,128)(2,1)S(1)} collective-permute-done((bf16[160,128]{1,0:T(8,128)(2,1)S(1)}, bf16[160,128]{1,0:T(8,128)(2,1)S(1)}, u32[]{:S(2)}, u32[]{:S(2)}) %collective-permute-start.3) | collective-permute-done | bytes 40992 | tf_op jit(solution)/shard_map/ppermute | solution.py:527
  27.5 0.3 middle_kernel.1
  27.8 0.7 pack_kernel.1
  28.5 0.0 copy-start.2
  28.5 0.0 copy-start.3
  28.5 28.3 %all_to_all.15.mine.arrived = bf16[32,32,128]{2,1,0:T(8,128)(2,1)S(1)} all-to-all(bf16[32,32,128]{2,1,0:T(8,128)(2,1)S(1)} %get-tuple-element.32), channel_id=1, replica_groups=mesh['gx'=4,'gy'=4,'gz'=32] {'gz'}, dimensions={0} | all-to-all | bytes 524288 | tf_op jit(solution)/shard_map/all_to_all | solution.py:537
  56.9 2.2 %partial_modes_kernel.1 = bf16[16,80,128]{2,1,0:T(8,128)(2,1)} custom-call(bf16[32,32,128]{2,1,0:T(8,128)(2,1)S(1)} %all_to_all.15.mine.arrived, f32[32,1024]{1,0:T(8,128)S(1)} %copy-done.3, bf16[128,1024]{1,0:T(8,128)(2,1)S(1)} %copy-done.2), custom_call_target="tpu_custom_call" | custom-call | tf_op jit(solution)/shard_map/partial_modes_kernel/pallas_call | solution.py:540
  59.1 6.0 %all-to-all-start.2 = ((bf16[16,80,128]{2,1,0:T(8,128)(2,1)}), bf16[16,80,128]{2,1,0:T(8,128)(2,1)S(1)}, u32[]{:S(2)}, u32[]{:S(2)}) async-start(bf16[16,80,128]{2,1,0:T(8,128)(2,1)} %partial_modes_kernel.1), calls=%async_computation.2 | async-start | bytes 655360 | tf_op jit(solution)/shard_map/all_to_all | solution.py:548
  65.1 2.0 %collective-permute-start.4 = (bf16[32,32,128]{2,1,0:T(8,128)(2,1)S(1)}, bf16[32,32,128]{2,1,0:T(8,128)(2,1)S(1)}, u32[]{:S(2)}, u32[]{:S(2)}) collective-permute-start(bf16[32,32,128]{2,1,0:T(8,128)(2,1)S(1)} %all_to_all.15.mine.arrived), channel_id=1, source_target_pairs={{0,32},{32,0},{64,96},{96,64},{1,33},{33,1},{65,97},{97,65},{2,34}... | collective-permute-start | bytes 786440 | tf_op jit(solution)/shard_map/ppermute | solution.py:538
  67.2 1.4 %collective-permute-done.4.other = bf16[32,32,128]{2,1,0:T(8,128)(2,1)S(1)} collective-permute-done((bf16[32,32,128]{2,1,0:T(8,128)(2,1)S(1)}, bf16[32,32,128]{2,1,0:T(8,128)(2,1)S(1)}, u32[]{:S(2)}, u32[]{:S(2)}) %collective-permute-start.4) | collective-permute-done | bytes 262176 | tf_op jit(solution)/shard_map/ppermute | solution.py:538
  68.6 2.0 %source_kernel.1 = f32[10,4,8,128]{3,2,1,0:T(8,128)} custom-call(s32[1]{0:T(128)} %bitcast.core.spot, s32[8]{0:T(128)S(1)} %bitcast.15, bf16[32,32,128]{2,1,0:T(8,128)(2,1)S(1)} %all_to_all.15.mine.arrived, bf16[32,32,128]{2,1,0:T(8,128)(2,1)S(1)} %collective-permute-done.4.other, bf16[8,64,128]{2,1,0:T(8,128)(2,1)S(1)} %get-tuple-element.33.high, ...), custom_call_target="tpu_custom_call" | custom-call | tf_op jit(solution)/shard_map/source_kernel/pallas_call | solution.py:549
  70.5 2.3 %all-to-all-done.2.arrived = bf16[16,80,128]{2,1,0:T(8,128)(2,1)S(1)} async-done(((bf16[16,80,128]{2,1,0:T(8,128)(2,1)}), bf16[16,80,128]{2,1,0:T(8,128)(2,1)S(1)}, u32[]{:S(2)}, u32[]{:S(2)}) %all-to-all-start.2) | async-done | bytes 327712 | tf_op jit(solution)/shard_map/all_to_all | solution.py:548
  72.8 0.7 sum_modes_kernel.1
  (19 shorter events, 0.0 us)
Async XLA Ops:
  0.6 7.3 %copy-start.1 = (f32[10,4,8,128]{3,2,1,0:T(8,128)S(1)}, f32[10,4,8,128]{3,2,1,0:T(8,128)}, u32[]{:S(2)}) copy-start(f32[10,4,8,128]{3,2,1,0:T(8,128)} %p.3) | copy-start | bytes 491524
  1.6 6.3 %copy-start = (f32[10,4,8,128]{3,2,1,0:T(8,128)S(1)}, f32[10,4,8,128]{3,2,1,0:T(8,128)}, u32[]{:S(2)}) copy-start(f32[10,4,8,128]{3,2,1,0:T(8,128)} %h.5) | copy-start | bytes 491524
  1.6 9.5 %collective-permute-start = (bf16[160,128]{1,0:T(8,128)(2,1)S(1)}, bf16[160,128]{1,0:T(8,128)(2,1)S(1)}, u32[]{:S(2)}, u32[]{:S(2)}) collective-permute-start(bf16[160,128]{1,0:T(8,128)(2,1)S(1)} %bitcast.18), channel_id=1, source_target_pairs={{0,1},{1,2},{2,3},{3,4},{4,5},{5,6},{6,7},{7,8},{8,9},{9,10},{10,1... | collective-permute-start | bytes 122888 | tf_op jit(solution)/shard_map/ppermute | solution.py:479
  6.6 5.4 %collective-permute-start.1 = (bf16[160,128]{1,0:T(8,128)(2,1)S(1)}, bf16[160,128]{1,0:T(8,128)(2,1)S(1)}, u32[]{:S(2)}, u32[]{:S(2)}) collective-permute-start(bf16[160,128]{1,0:T(8,128)(2,1)S(1)} %bitcast.17), channel_id=1, source_target_pairs={{1,0},{2,1},{3,2},{4,3},{5,4},{6,5},{7,6},{8,7},{9,8},{10,9},{11,1... | collective-permute-start | bytes 122888 | tf_op jit(solution)/shard_map/ppermute | solution.py:480
  7.9 0.7 copy-start.4
  7.9 0.7 copy-start.6
  8.6 1.8 %copy-start.5 = (f32[1,10,8,64]{3,2,1,0:T(8,128)S(1)}, f32[1,10,8,64]{3,2,1,0:T(8,128)}, u32[]{:S(2)}) copy-start(f32[1,10,8,64]{3,2,1,0:T(8,128)} %param.20) | copy-start | bytes 61444
  8.6 1.8 %copy-start.7 = (f32[1,1,1,8,3,128]{5,3,4,2,1,0:T(8,128)S(1)}, f32[1,1,1,8,3,128]{5,3,4,2,1,0:T(8,128)}, u32[]{:S(2)}) copy-start(f32[1,1,1,8,3,128]{5,3,4,2,1,0:T(8,128)} %param.18) | copy-start | bytes 36868
  8.6 1.8 %copy-start.10 = (f32[3,128]{1,0:T(4,128)S(1)}, f32[3,128]{1,0:T(4,128)}, u32[]{:S(2)}) copy-start(f32[3,128]{1,0:T(4,128)} %frac.1) | copy-start | bytes 4612
  10.3 0.7 copy-start.8
  10.4 0.7 copy-start.9
  10.4 0.7 copy-start.11
  10.4 0.7 copy-start.12
  12.9 14.9 %all-to-all-start = ((bf16[16,16,128]{2,1,0:T(8,128)(2,1)}), bf16[16,16,128]{2,1,0:T(8,128)(2,1)S(1)}, u32[]{:S(2)}, u32[]{:S(2)}) async-start(bf16[16,16,128]{2,1,0:T(8,128)(2,1)} %get-tuple-element.28), calls=%async_computation | async-start | bytes 131072 | tf_op jit(solution)/shard_map/all_to_all | solution.py:524
  20.1 5.6 %collective-permute-start.2 = (bf16[160,128]{1,0:T(8,128)(2,1)S(1)}, bf16[160,128]{1,0:T(8,128)(2,1)S(1)}, u32[]{:S(2)}, u32[]{:S(2)}) collective-permute-start(bf16[160,128]{1,0:T(8,128)(2,1)S(1)} %get-tuple-element.24), channel_id=1, source_target_pairs={{0,32},{32,0},{64,96},{96,64},{1,33},{33,1},{65,97},{97,65},{2,34}... | collective-permute-start | bytes 122888 | tf_op jit(solution)/shard_map/ppermute | solution.py:526
  22.2 5.3 %collective-permute-start.3 = (bf16[160,128]{1,0:T(8,128)(2,1)S(1)}, bf16[160,128]{1,0:T(8,128)(2,1)S(1)}, u32[]{:S(2)}, u32[]{:S(2)}) collective-permute-start(bf16[160,128]{1,0:T(8,128)(2,1)S(1)} %get-tuple-element.25), channel_id=1, source_target_pairs={{32,64},{64,32},{33,65},{65,33},{34,66},{66,34},{35,67},{67,35},{3... | collective-permute-start | bytes 122888 | tf_op jit(solution)/shard_map/ppermute | solution.py:527
  28.5 28.4 %copy-start.2 = (bf16[128,1024]{1,0:T(8,128)(2,1)S(1)}, bf16[128,1024]{1,0:T(8,128)(2,1)}, u32[]{:S(2)}) copy-start(bf16[128,1024]{1,0:T(8,128)(2,1)} %constant.36.clone.angular) | copy-start | bytes 786436
  28.5 28.4 %copy-start.3 = (f32[32,1024]{1,0:T(8,128)S(1)}, f32[32,1024]{1,0:T(8,128)}, u32[]{:S(2)}) copy-start(f32[32,1024]{1,0:T(8,128)} %constant.35.clone.radial) | copy-start | bytes 393220
  59.1 13.7 %all-to-all-start.2 = ((bf16[16,80,128]{2,1,0:T(8,128)(2,1)}), bf16[16,80,128]{2,1,0:T(8,128)(2,1)S(1)}, u32[]{:S(2)}, u32[]{:S(2)}) async-start(bf16[16,80,128]{2,1,0:T(8,128)(2,1)} %partial_modes_kernel.1), calls=%async_computation.2 | async-start | bytes 655360 | tf_op jit(solution)/shard_map/all_to_all | solution.py:548
  65.1 3.4 %collective-permute-start.4 = (bf16[32,32,128]{2,1,0:T(8,128)(2,1)S(1)}, bf16[32,32,128]{2,1,0:T(8,128)(2,1)S(1)}, u32[]{:S(2)}, u32[]{:S(2)}) collective-permute-start(bf16[32,32,128]{2,1,0:T(8,128)(2,1)S(1)} %all_to_all.15.mine.arrived), channel_id=1, source_target_pairs={{0,32},{32,0},{64,96},{96,64},{1,33},{33,1},{65,97},{97,65},{2,34}... | collective-permute-start | bytes 786440 | tf_op jit(solution)/shard_map/ppermute | solution.py:538
